TPU v7x, 32 devices: a whole 2x2x4 slice. The times are simulated.
32 devices in a mesh: tm: 16 (over z, y, x), tile: 2 (over core).
Axes of the slice: x: 2, y: 2, z: 4, core: 2. Of those that a mesh axis runs over, the one named last changes fastest.
Arguments:
- latent: bfloat16 [64, 8, 160, 128], P('tm', 'tile'), may hold values from -6 to 6
- cot_forward: bfloat16 [64, 8, 160, 128], P('tm', 'tile'), may hold values from -6 to 6
- cot_reverse: bfloat16 [64, 8, 160, 128], P('tm', 'tile'), may hold values from -6 to 6
- spatial_weight: bfloat16 [3, 3, 128, 128], replicated, may hold values from -0.1875 to 0.1875
- temporal_weight: bfloat16 [3, 128, 128], replicated, may hold values from -0.3125 to 0.3125
Outputs:
- out_forward: bfloat16 [64, 8, 160, 128], P('tm', 'tile')
- out_reverse: bfloat16 [64, 8, 160, 128], P('tm', 'tile')
- grad_input: bfloat16 [64, 8, 160, 128], P('tm', 'tile')
- grad_spatial: float32 [3, 3, 128, 128], replicated
- grad_temporal: float32 [3, 128, 128], replicated
All inputs are finite; a program needn't handle non-finite values.
Results may differ from a plain program's by a relative error of at most 0.0032.
Values may be sent and summed in bfloat16 or wider, within the bound.
A program may use at most 64 MiB of HBM per device.

v0:
```python
import math

import jax
import jax.numpy as jnp
from jax import lax
from jax.sharding import PartitionSpec as P


def extended_2(cells, sides, width):
    for axis, dim in sides:
        count = lax.axis_size(axis)
        ends = count - 1
        head = lax.slice_in_dim(cells, 0, width, axis=dim)
        tail = lax.slice_in_dim(cells, cells.shape[dim] - width, cells.shape[dim], axis=dim)
        cells = jnp.concatenate(
            [
                lax.ppermute(tail, axis, [(i, (i + 1) % count) for i in range(ends)]),
                cells,
                lax.ppermute(head, axis, [((i + 1) % count, i) for i in range(ends)]),
            ],
            axis=dim,
        )
    return cells


def shifted(value, axis, steps):
    count = lax.axis_size(axis)
    initial, last = (max(0, -steps), min(count, count - steps))
    return lax.ppermute(value, axis, [(source, source + steps) for source in range(initial, last)])


def spatial_rows(padded, height, width_cells, flipped):
    pieces = []
    for row_step in range(3):
        for col_step in range(3):
            row_from = 2 - row_step if flipped else row_step
            col_from = 2 - col_step if flipped else col_step
            pieces.append(
                padded[:, row_from : row_from + height, col_from : col_from + width_cells, :]
            )
    joined = jnp.concatenate(pieces, axis=3)
    return joined.reshape(-1, joined.shape[3])


def widen(values):
    return jnp.pad(values, ((0, 0), (0, 0), (1, 1), (0, 0)))


def temporal_rows(extended, offsets, frame_count):
    joined = jnp.concatenate(
        [extended[offset : offset + frame_count] for offset in offsets], axis=2
    )
    return joined.reshape(-1, joined.shape[2])


def contract_rows(left, right):
    return lax.dot_general(
        left, right, (((0,), (0,)), ((), ())), preferred_element_type=jnp.float32
    )


def body(latent, cot_forward, cot_reverse, spatial_weight, temporal_weight):
    frame_count, height, width_cells, channels = latent.shape
    plane_cells = height * width_cells
    spatial_flat = spatial_weight.reshape(9 * channels, channels)
    flipped_flat = jnp.transpose(spatial_weight, (0, 1, 3, 2)).reshape(9 * channels, channels)
    forward_flat = temporal_weight.reshape(3 * channels, channels)
    backward_flat = jnp.transpose(temporal_weight, (0, 2, 1)).reshape(3 * channels, channels)
    latent_flat = latent.reshape(-1, channels)
    fwd_cot = cot_forward.reshape(frame_count, plane_cells, channels)
    rev_cot = cot_reverse.reshape(frame_count, plane_cells, channels)
    rimmed = extended_2(latent, (("tile", 1),), 1)
    patches = spatial_rows(widen(rimmed), height, width_cells, False)
    pre_act = jnp.dot(patches, spatial_flat, preferred_element_type=jnp.float32)
    act_frames = (
        jax.nn.silu(pre_act).astype(jnp.bfloat16).reshape(frame_count, plane_cells, channels)
    )
    rimmed_act = extended_2(act_frames, (("tm", 0),), 2)
    following = shifted(fwd_cot[:2], "tm", -1)
    earlier = shifted(rev_cot[-2:], "tm", 1)
    causal = temporal_rows(rimmed_act, (2, 1, 0), frame_count)
    anticausal = temporal_rows(rimmed_act, (2, 3, 4), frame_count)
    residual_in = latent_flat.astype(jnp.float32)
    out_forward = (
        (residual_in + jnp.dot(causal, forward_flat, preferred_element_type=jnp.float32))
        .astype(jnp.bfloat16)
        .reshape(latent.shape)
    )
    out_reverse = (
        (residual_in + jnp.dot(anticausal, forward_flat, preferred_element_type=jnp.float32))
        .astype(jnp.bfloat16)
        .reshape(latent.shape)
    )
    ahead_rows = temporal_rows(
        jnp.concatenate([fwd_cot, following], axis=0), (0, 1, 2), frame_count
    )
    behind = temporal_rows(jnp.concatenate([earlier, rev_cot], axis=0), (2, 1, 0), frame_count)
    grad_act = jnp.dot(ahead_rows, backward_flat, preferred_element_type=jnp.float32)
    grad_act = grad_act + jnp.dot(behind, backward_flat, preferred_element_type=jnp.float32)
    grad_temp = contract_rows(causal, cot_forward.reshape(-1, channels))
    grad_temp = grad_temp + contract_rows(anticausal, cot_reverse.reshape(-1, channels))
    sigmoid_pre = jax.nn.sigmoid(pre_act)
    grad_pre = (grad_act * sigmoid_pre * (1.0 + pre_act * (1.0 - sigmoid_pre))).astype(jnp.bfloat16)
    grad_rim = extended_2(grad_pre.reshape(latent.shape), (("tile", 1),), 1)
    grad_patches = spatial_rows(widen(grad_rim), height, width_cells, True)
    total_in = cot_forward.reshape(-1, channels).astype(jnp.float32) + cot_reverse.reshape(
        -1, channels
    ).astype(jnp.float32)
    total_in = total_in + jnp.dot(grad_patches, flipped_flat, preferred_element_type=jnp.float32)
    grad_input = total_in.astype(jnp.bfloat16).reshape(latent.shape)
    grad_space = contract_rows(patches, grad_pre)
    grad_space, grad_temp = lax.psum((grad_space, grad_temp), ("tm", "tile"))
    positions = frame_count * height * width_cells * lax.axis_size("tm") * lax.axis_size("tile")
    grad_scale = 1.0 / math.sqrt(positions)
    grad_spatial = (grad_space * grad_scale).reshape(3, 3, channels, channels)
    grad_temporal = (grad_temp * grad_scale).reshape(3, channels, channels)
    return (out_forward, out_reverse, grad_input, grad_spatial, grad_temporal)


def solution(mesh):
    placed = (
        P("tm", "tile", None, None),
        P("tm", "tile", None, None),
        P("tm", "tile", None, None),
        P(),
        P(),
    )
    return jax.shard_map(
        body,
        mesh=mesh,
        in_specs=placed,
        out_specs=(
            P("tm", "tile", None, None),
            P("tm", "tile", None, None),
            P("tm", "tile", None, None),
            P(),
            P(),
        ),
        check_vma=False,
    )
```

profile of v0, /device:TPU:0, one launch (start us, length us, event | category | flops | bytes accessed | tf_op | source)
XLA Modules:
  0.0 196.7 jit_solution(5364787009995814116)
XLA Ops:
  7.2 1.1 fusion.41
  8.3 2.4 %collective-permute-start = (bf16[4,1,160,128]{3,2,1,0:T(8,128)(2,1)S(1)}, bf16[4,1,160,128]{3,2,1,0:T(8,128)(2,1)S(1)}, u32[]{:S(2)}, u32[]{:S(2)}) collective-permute-start(bf16[4,1,160,128]{3,2,1,0:T(8,128)(2,1)S(1)} %get-tuple-element.29), channel_id=1, source_target_pairs={{0,1},{2,3},{4,5},{6,7},{8,9},{10,11},{12,13},{14,15},{16,17},{18,... | collective-permute-start | bytes 491528 | tf_op jit(solution)/shard_map/ppermute | solution.py:17
  10.7 1.3 collective-permute-start.1
  12.0 1.0 slice.146
  13.0 4.2 %collective-permute-start.5 = (bf16[2,640,128]{2,1,0:T(8,128)(2,1)S(1)}, bf16[2,640,128]{2,1,0:T(8,128)(2,1)S(1)}, u32[]{:S(2)}, u32[]{:S(2)}) collective-permute-start(bf16[2,640,128]{2,1,0:T(8,128)(2,1)S(1)} %bitcast.91), channel_id=1, source_target_pairs={{0,2},{2,4},{4,6},{6,8},{8,10},{10,12},{12,14},{14,16},{16,18},{18... | collective-permute-start | bytes 983048 | tf_op jit(solution)/shard_map/ppermute | solution.py:29
  17.3 1.0 slice.142
  18.3 1.3 collective-permute-start.4
  19.6 1.0 copy.10
  20.6 1.9 copy.11
  22.5 1.4 select_maximum_fusion.2
  25.6 1.8 multiply_convert_fusion
  27.5 4.6 %collective-permute-start.2 = (bf16[2,640,128]{2,1,0:T(8,128)(2,1)S(1)}, bf16[2,640,128]{2,1,0:T(8,128)(2,1)S(1)}, u32[]{:S(2)}, u32[]{:S(2)}) collective-permute-start(bf16[2,640,128]{2,1,0:T(8,128)(2,1)S(1)} %bitcast.90), channel_id=1, source_target_pairs={{0,2},{2,4},{4,6},{6,8},{8,10},{10,12},{12,14},{14,16},{16,18},{18... | collective-permute-start | bytes 983048 | tf_op jit(solution)/shard_map/ppermute | solution.py:17
  32.1 1.3 collective-permute-start.3
  36.2 2.0 %collective-permute-start.6 = (bf16[4,1,160,128]{3,2,1,0:T(8,128)(2,1)S(1)}, bf16[4,1,160,128]{3,2,1,0:T(8,128)(2,1)S(1)}, u32[]{:S(2)}, u32[]{:S(2)}) collective-permute-start(bf16[4,1,160,128]{3,2,1,0:T(8,128)(2,1)S(1)} %get-tuple-element.23), channel_id=1, source_target_pairs={{0,1},{2,3},{4,5},{6,7},{8,9},{10,11},{12,13},{14,15},{16,17},{18,... | collective-permute-start | bytes 491528 | tf_op jit(solution)/shard_map/ppermute | solution.py:17
  38.2 1.5 collective-permute-start.7
  39.7 2.6 %fusion.42 = f32[1152,128]{1,0:T(8,128)} fusion(bf16[2560,1152]{1,0:T(8,128)(2,1)S(1)} %bitcast.101, bf16[2560,128]{1,0:T(8,128)(2,1)S(1)} %fusion.5), kind=kOutput, calls=%fused_computation.87 | convolution fusion | flops 754974720 | bytes 7143424 | tf_op jit(solution)/shard_map/dot_general | solution.py:57
  42.6 1.4 fusion.38
  43.9 0.9 constant_dynamic-update-slice_fusion.9
  45.0 0.9 constant_dynamic-update-slice_fusion.8
  45.9 0.9 constant_dynamic-update-slice_fusion.7
  47.8 1.0 constant_dynamic-update-slice_fusion.5
  51.3 1.4 convolution_add_fusion.4
  52.8 2.1 %constant_dynamic-update-slice_fusion.4 = bf16[2560,1152]{1,0:T(8,128)(2,1)} fusion(bf16[2560,1152]{1,0:T(8,128)(2,1)} %constant_dynamic-update-slice_fusion.5, bf16[2560,128]{1,0:T(8,128)(2,1)} %bitcast.64), kind=kLoop, calls=%fused_computation.71 | loop fusion | bytes 1310720
  54.9 0.9 constant_dynamic-update-slice_fusion.3
  55.9 1.0 constant_dynamic-update-slice_fusion.2
  56.8 0.9 constant_dynamic-update-slice_fusion.1
  57.8 5.3 %fusion.4 = bf16[2560,128]{1,0:T(8,128)(2,1)} fusion(bf16[2560,1152]{1,0:T(8,128)(2,1)} %constant_dynamic-update-slice_fusion.1, bf16[1152,128]{1,0:T(8,128)(2,1)S(1)} %bitcast.94, bf16[2560,128]{1,0:T(8,128)(2,1)S(1)} %bitcast.75, bf16[2560,128]{1,0:T(8,128)(2,1)S(1)} %bitcast.71), kind=kOutput, calls=%fused_computation.8 | convolution fusion | flops 756613120 | bytes 8159232 | tf_op jit(solution)/shard_map/dot_general | solution.py:109
  63.2 1.5 fusion.3
  64.7 1.5 fusion.2
  66.2 120.0 %all-reduce.5.cloned.1.call-done = (f32[1152,128]{1,0:T(8,128)}, f32[384,128]{1,0:T(8,128)}) async-done(((f32[1152,128]{1,0:T(8,128)}, f32[384,128]{1,0:T(8,128)}), (f32[1152,128]{1,0:T(8,128)}, f32[384,128]{1,0:T(8,128)})) %all-reduce.5.cloned.1.call-update) | async-done | bytes 786448 | tf_op jit(solution)/shard_map/psum | solution.py:112
  186.3 1.9 broadcast_multiply_fusion
  188.2 1.6 broadcast_multiply_fusion.1
  (62 shorter events, 8.4 us)
Async XLA Ops:
  7.2 16.8 %copy-start = (bf16[4,4,160,128]{3,2,1,0:T(8,128)(2,1)S(1)}, bf16[4,4,160,128]{3,2,1,0:T(8,128)(2,1)}, u32[]{:S(2)}) copy-start(bf16[4,4,160,128]{3,2,1,0:T(8,128)(2,1)} %param.5) | copy-start | bytes 1966084
  7.2 179.1 %all-reduce.5.cloned.1.call-start = ((), (), s32[]{:S(2)}) async-start(), calls=%async_computation | async-start | bytes 1572864 | tf_op jit(solution)/shard_map/psum | solution.py:112
  8.3 14.1 %collective-permute-start = (bf16[4,1,160,128]{3,2,1,0:T(8,128)(2,1)S(1)}, bf16[4,1,160,128]{3,2,1,0:T(8,128)(2,1)S(1)}, u32[]{:S(2)}, u32[]{:S(2)}) collective-permute-start(bf16[4,1,160,128]{3,2,1,0:T(8,128)(2,1)S(1)} %get-tuple-element.29), channel_id=1, source_target_pairs={{0,1},{2,3},{4,5},{6,7},{8,9},{10,11},{12,13},{14,15},{16,17},{18,... | collective-permute-start | bytes 491528 | tf_op jit(solution)/shard_map/ppermute | solution.py:17
  10.7 11.7 %collective-permute-start.1 = (bf16[4,1,160,128]{3,2,1,0:T(8,128)(2,1)S(1)}, bf16[4,1,160,128]{3,2,1,0:T(8,128)(2,1)S(1)}, u32[]{:S(2)}, u32[]{:S(2)}) collective-permute-start(bf16[4,1,160,128]{3,2,1,0:T(8,128)(2,1)S(1)} %get-tuple-element.30), channel_id=1, source_target_pairs={{1,0},{3,2},{5,4},{7,6},{9,8},{11,10},{13,12},{15,14},{17,16},{19,... | collective-permute-start | bytes 491528 | tf_op jit(solution)/shard_map/ppermute | solution.py:19
  13.0 21.9 %collective-permute-start.5 = (bf16[2,640,128]{2,1,0:T(8,128)(2,1)S(1)}, bf16[2,640,128]{2,1,0:T(8,128)(2,1)S(1)}, u32[]{:S(2)}, u32[]{:S(2)}) collective-permute-start(bf16[2,640,128]{2,1,0:T(8,128)(2,1)S(1)} %bitcast.91), channel_id=1, source_target_pairs={{0,2},{2,4},{4,6},{6,8},{8,10},{10,12},{12,14},{14,16},{16,18},{18... | collective-permute-start | bytes 983048 | tf_op jit(solution)/shard_map/ppermute | solution.py:29
  18.3 15.9 %collective-permute-start.4 = (bf16[2,640,128]{2,1,0:T(8,128)(2,1)S(1)}, bf16[2,640,128]{2,1,0:T(8,128)(2,1)S(1)}, u32[]{:S(2)}, u32[]{:S(2)}) collective-permute-start(bf16[2,640,128]{2,1,0:T(8,128)(2,1)S(1)} %bitcast.92), channel_id=1, source_target_pairs={{2,0},{4,2},{6,4},{8,6},{10,8},{12,10},{14,12},{16,14},{18,16},{20... | collective-permute-start | bytes 983048 | tf_op jit(solution)/shard_map/ppermute | solution.py:29
  24.4 1.2 copy-start.13
  25.6 8.5 %copy-start.1 = (bf16[4,4,160,128]{3,2,1,0:T(8,128)(2,1)S(1)}, bf16[4,4,160,128]{3,2,1,0:T(8,128)(2,1)}, u32[]{:S(2)}) copy-start(bf16[4,4,160,128]{3,2,1,0:T(8,128)(2,1)} %param.6) | copy-start | bytes 1966084
  27.5 21.3 %collective-permute-start.2 = (bf16[2,640,128]{2,1,0:T(8,128)(2,1)S(1)}, bf16[2,640,128]{2,1,0:T(8,128)(2,1)S(1)}, u32[]{:S(2)}, u32[]{:S(2)}) collective-permute-start(bf16[2,640,128]{2,1,0:T(8,128)(2,1)S(1)} %bitcast.90), channel_id=1, source_target_pairs={{0,2},{2,4},{4,6},{6,8},{8,10},{10,12},{12,14},{14,16},{16,18},{18... | collective-permute-start | bytes 983048 | tf_op jit(solution)/shard_map/ppermute | solution.py:17
  32.1 17.5 %collective-permute-start.3 = (bf16[2,640,128]{2,1,0:T(8,128)(2,1)S(1)}, bf16[2,640,128]{2,1,0:T(8,128)(2,1)S(1)}, u32[]{:S(2)}, u32[]{:S(2)}) collective-permute-start(bf16[2,640,128]{2,1,0:T(8,128)(2,1)S(1)} %bitcast.89), channel_id=1, source_target_pairs={{2,0},{4,2},{6,4},{8,6},{10,8},{12,10},{14,12},{16,14},{18,16},{20... | collective-permute-start | bytes 983048 | tf_op jit(solution)/shard_map/ppermute | solution.py:19
  34.1 1.1 copy-start.3
  36.2 6.1 %collective-permute-start.6 = (bf16[4,1,160,128]{3,2,1,0:T(8,128)(2,1)S(1)}, bf16[4,1,160,128]{3,2,1,0:T(8,128)(2,1)S(1)}, u32[]{:S(2)}, u32[]{:S(2)}) collective-permute-start(bf16[4,1,160,128]{3,2,1,0:T(8,128)(2,1)S(1)} %get-tuple-element.23), channel_id=1, source_target_pairs={{0,1},{2,3},{4,5},{6,7},{8,9},{10,11},{12,13},{14,15},{16,17},{18,... | collective-permute-start | bytes 491528 | tf_op jit(solution)/shard_map/ppermute | solution.py:17
  38.2 4.1 %collective-permute-start.7 = (bf16[4,1,160,128]{3,2,1,0:T(8,128)(2,1)S(1)}, bf16[4,1,160,128]{3,2,1,0:T(8,128)(2,1)S(1)}, u32[]{:S(2)}, u32[]{:S(2)}) collective-permute-start(bf16[4,1,160,128]{3,2,1,0:T(8,128)(2,1)S(1)} %get-tuple-element.24), channel_id=1, source_target_pairs={{1,0},{3,2},{5,4},{7,6},{9,8},{11,10},{13,12},{15,14},{17,16},{19,... | collective-permute-start | bytes 491528 | tf_op jit(solution)/shard_map/ppermute | solution.py:19
  49.8 0.8 copy-start.9
  49.8 1.0 copy-start.11
  49.8 1.2 copy-start.5
  49.9 1.4 copy-start.7
  52.7 5.0 %copy-start.2 = (bf16[4,4,160,128]{3,2,1,0:T(8,128)(2,1)S(1)}, bf16[4,4,160,128]{3,2,1,0:T(8,128)(2,1)}, u32[]{:S(2)}) copy-start(bf16[4,4,160,128]{3,2,1,0:T(8,128)(2,1)} %param.6) | copy-start | bytes 1966084
  52.7 5.0 %copy-start.4 = (bf16[4,4,160,128]{3,2,1,0:T(8,128)(2,1)S(1)}, bf16[4,4,160,128]{3,2,1,0:T(8,128)(2,1)}, u32[]{:S(2)}) copy-start(bf16[4,4,160,128]{3,2,1,0:T(8,128)(2,1)} %param.7) | copy-start | bytes 1966084
  52.8 5.0 %copy-start.14 = (bf16[3,3,128,128]{2,3,1,0:T(8,128)(2,1)S(1)}, bf16[3,3,128,128]{2,3,1,0:T(8,128)(2,1)}, u32[]{:S(2)}) copy-start(bf16[3,3,128,128]{2,3,1,0:T(8,128)(2,1)} %copy.11) | copy-start | bytes 884740
  57.8 5.4 %copy-start.10 = (bf16[4,640,128]{2,1,0:T(8,128)(2,1)S(1)}, bf16[4,640,128]{2,1,0:T(8,128)(2,1)}, u32[]{:S(2)}) copy-start(bf16[4,640,128]{2,1,0:T(8,128)(2,1)} %copy-done.9) | copy-start | bytes 1966084
  57.8 5.4 %copy-start.12 = (bf16[4,640,128]{2,1,0:T(8,128)(2,1)S(1)}, bf16[4,640,128]{2,1,0:T(8,128)(2,1)}, u32[]{:S(2)}) copy-start(bf16[4,640,128]{2,1,0:T(8,128)(2,1)} %copy-done.11) | copy-start | bytes 1966084
  57.8 5.4 %copy-start.15 = (bf16[3,128,128]{2,1,0:T(8,128)(2,1)S(1)}, bf16[3,128,128]{2,1,0:T(8,128)(2,1)}, u32[]{:S(2)}) copy-start(bf16[3,128,128]{2,1,0:T(8,128)(2,1)} %param.9) | copy-start | bytes 294916
  63.2 1.5 copy-start.6
  63.2 1.5 copy-start.8
Sparse Core Ops, SparseCore 0:
  52.9 133.3 all-reduce.4
where the time goes:
time: 197 us
  waiting for transfers between devices  122 us (62%)
  local copies, waits for them, and re-layouts  19.6 us (10%)
  starting transfers between devices  18.6 us (9%)
  matrix products  16.4 us (8%)
  between operations  14.4 us (7%)
  other arithmetic  6.05 us (3%)
    psum x1, waiting for transfers between devices, body(): grad_space, grad_temp = lax.psum((grad_space, grad_temp), ('tm', 'tile'))  120 us
    unnamed x48, local copies, waits for them, and re-layouts  13.9 us
    ppermute x3, starting transfers between devices, extended_2(): lax.ppermute(tail, axis, [(i, (i + 1) % count) for i in range(ends)])  9 us
    ppermute x2, starting transfers between devices, shifted(): lax.ppermute(value, axis, [(source, source + steps) for source in range(i...  5.53 us
    dot_general x1, matrix products, body(): jnp.dot(grad_patches, flipped_flat, preferred_element_type=jnp.float32)  5.35 us
    dot_general x3, matrix products, contract_rows(): lax.dot_general(left, right, (((0,), (0,)), ((), ())), preferred_element_...  4.68 us
    ppermute x3, starting transfers between devices, extended_2(): lax.ppermute(head, axis, [((i + 1) % count, i) for i in range(ends)])  4.06 us
  transfers between devices with their start and end apart: 9, of which 3 were waited for; matrix products, arithmetic and copies ran while one was open for 17% of the time, Pallas kernels for 0%

commit v1 on v0

--- a/solution.py
+++ b/solution.py
@@ -1,8 +1,11 @@
+import functools
 import math
 
 import jax
 import jax.numpy as jnp
 from jax import lax
+from jax.experimental import pallas as pl
+from jax.experimental.pallas import tpu as pltpu
 from jax.sharding import PartitionSpec as P
 
 
@@ -59,6 +62,125 @@
     )
 
 
+MESH = pl.DeviceIdType.MESH
+
+
+def sum_kernel(tiles, shards, scale, x_ref, o_ref, pair_in, mid, shard_in, send_sem, recv_sem):
+    tile, shard = lax.axis_index("tile"), lax.axis_index("tm")
+    rows = x_ref.shape[0]
+    half = rows // tiles
+    chunk = half // shards
+
+    def tile_peer(step):
+        return lax.rem(tile + step, tiles)
+
+    def shard_peer(step):
+        return lax.rem(shard + step, shards)
+
+    def at(start, size):
+        return pl.ds(pl.multiple_of(start, 8), size)
+
+    def each(count, act):
+        def step(index, carry):
+            act(index)
+            return carry
+
+        lax.fori_loop(1, count, step, 0)
+
+    def settle(phase, ref):
+        pltpu.make_async_copy(ref, ref, send_sem.at[phase]).wait()
+        pltpu.make_async_copy(ref, ref, recv_sem.at[phase]).wait()
+
+    def send(src, dst, phase, peer):
+        pltpu.make_async_remote_copy(
+            src_ref=src,
+            dst_ref=dst,
+            send_sem=send_sem.at[phase],
+            recv_sem=recv_sem.at[phase],
+            device_id=peer,
+            device_id_type=MESH,
+        ).start()
+
+    barrier = pltpu.get_barrier_semaphore()
+    each(
+        tiles,
+        lambda step: pl.semaphore_signal(
+            barrier, inc=1, device_id={"tile": tile_peer(step)}, device_id_type=MESH
+        ),
+    )
+    each(
+        shards,
+        lambda step: pl.semaphore_signal(
+            barrier, inc=1, device_id={"tm": shard_peer(step)}, device_id_type=MESH
+        ),
+    )
+    pl.semaphore_wait(barrier, tiles + shards - 2)
+
+    each(
+        tiles,
+        lambda step: send(
+            x_ref.at[at(tile_peer(step) * half, half)],
+            pair_in.at[step - 1],
+            0,
+            {"tile": tile_peer(step)},
+        ),
+    )
+    settle(0, pair_in)
+    total = x_ref[at(tile * half, half), :]
+    for index in range(tiles - 1):
+        total = total + pair_in[index]
+    mid[...] = total
+    each(
+        shards,
+        lambda step: send(
+            mid.at[at(shard_peer(step) * chunk, chunk)],
+            shard_in.at[step - 1],
+            1,
+            {"tm": shard_peer(step)},
+        ),
+    )
+    settle(1, shard_in)
+    part = lax.fori_loop(
+        0,
+        shards - 1,
+        lambda index, value: value + shard_in[index],
+        mid[at(shard * chunk, chunk), :],
+    )
+    own = at(tile * half + shard * chunk, chunk)
+    o_ref[own, :] = part * scale
+    each(shards, lambda step: send(o_ref.at[own], o_ref.at[own], 2, {"tm": shard_peer(step)}))
+    settle(2, o_ref.at[pl.ds(0, (shards - 1) * chunk)])
+    mine = at(tile * half, half)
+    each(tiles, lambda step: send(o_ref.at[mine], o_ref.at[mine], 3, {"tile": tile_peer(step)}))
+    settle(3, o_ref.at[pl.ds(0, (tiles - 1) * half)])
+
+
+def summed(values, scale):
+    tiles, shards = lax.axis_size("tile"), lax.axis_size("tm")
+    rows, channels = values.shape
+    unit = 8 * tiles * shards
+    padded = -(-rows // unit) * unit
+    if padded > rows:
+        values = jnp.pad(values, ((0, padded - rows), (0, 0)))
+    half = padded // tiles
+    chunk = half // shards
+    out = pl.pallas_call(
+        functools.partial(sum_kernel, tiles, shards, scale),
+        out_shape=jax.ShapeDtypeStruct(values.shape, jnp.float32),
+        in_specs=[pl.BlockSpec(memory_space=pltpu.VMEM)],
+        out_specs=pl.BlockSpec(memory_space=pltpu.VMEM),
+        scratch_shapes=[
+            pltpu.VMEM((tiles - 1, half, channels), jnp.float32),
+            pltpu.VMEM((half, channels), jnp.float32),
+            pltpu.VMEM((shards - 1, chunk, channels), jnp.float32),
+            pltpu.SemaphoreType.DMA((4,)),
+            pltpu.SemaphoreType.DMA((4,)),
+        ],
+        compiler_params=pltpu.CompilerParams(collective_id=0, has_side_effects=True),
+    )(values)
+    return out[:rows]
+
+
 def body(latent, cot_forward, cot_reverse, spatial_weight, temporal_weight):
     frame_count, height, width_cells, channels = latent.shape
     plane_cells = height * width_cells
@@ -109,11 +231,11 @@
     total_in = total_in + jnp.dot(grad_patches, flipped_flat, preferred_element_type=jnp.float32)
     grad_input = total_in.astype(jnp.bfloat16).reshape(latent.shape)
     grad_space = contract_rows(patches, grad_pre)
-    grad_space, grad_temp = lax.psum((grad_space, grad_temp), ("tm", "tile"))
     positions = frame_count * height * width_cells * lax.axis_size("tm") * lax.axis_size("tile")
     grad_scale = 1.0 / math.sqrt(positions)
-    grad_spatial = (grad_space * grad_scale).reshape(3, 3, channels, channels)
-    grad_temporal = (grad_temp * grad_scale).reshape(3, channels, channels)
+    grads = summed(jnp.concatenate([grad_space, grad_temp], axis=0), grad_scale)
+    grad_spatial = grads[: 9 * channels].reshape(3, 3, channels, channels)
+    grad_temporal = grads[9 * channels :].reshape(3, channels, channels)
     return (out_forward, out_reverse, grad_input, grad_spatial, grad_temporal)
 
 

time: 197 us -> 91.2 us (0.46)
  the two profiles are of different devices: /device:TPU:0 before, /device:TPU:25 now
where the time goes in v1:
time: 91.2 us; the launch traced here: 90.6 us
  Pallas kernels  30.8 us (34%)
  starting transfers between devices  23.5 us (26%)
  local copies, waits for them, and re-layouts  14.8 us (16%)
  matrix products  13.5 us (15%)
  other arithmetic  5.31 us (6%)
  waiting for transfers between devices  1.58 us (2%)
  between operations  1.09 us (1%)
    pallas_call x1, Pallas kernels, summed(): pl.pallas_call(functools.partial(sum_kernel, tiles, shards, scale), out_s...  30.8 us
    ppermute x3, starting transfers between devices, extended_2(): lax.ppermute(head, axis, [((i + 1) % count, i) for i in range(ends)])  11.9 us
    ppermute x2, starting transfers between devices, shifted(): lax.ppermute(value, axis, [(source, source + steps) for source in range(i...  7.07 us
    unnamed x40, local copies, waits for them, and re-layouts  5.52 us
    ppermute x3, starting transfers between devices, extended_2(): lax.ppermute(tail, axis, [(i, (i + 1) % count) for i in range(ends)])  4.49 us
    concatenate x4, other arithmetic, extended_2(): jnp.concatenate([lax.ppermute(tail, axis, [(i, (i + 1) % count) for i in...  3.88 us
    dot_general x3, matrix products, contract_rows(): lax.dot_general(left, right, (((0,), (0,)), ((), ())), preferred_element_...  3.17 us
    dot_general x1, matrix products, body(): jnp.dot(anticausal, forward_flat, preferred_element_type=jnp.float32)  2.8 us
  transfers between devices with their start and end apart: 8, of which 1 were waited for; matrix products, arithmetic and copies ran while one was open for 28% of the time, Pallas kernels for 34%

profile of v1, /device:TPU:25, one launch (start us, length us, event | category | flops | bytes accessed | tf_op | source)
XLA Modules:
  0.0 90.6 jit_solution(14703628708199046930)
XLA Ops:
  0.6 1.1 %fusion.41 = (bf16[4,1,160,128]{3,2,1,0:T(8,128)(2,1)S(1)}, bf16[4,1,160,128]{3,2,1,0:T(8,128)(2,1)S(1)}) fusion(bf16[4,4,160,128]{3,2,1,0:T(8,128)(2,1)} %param.5), kind=kLoop, calls=%fused_computation.85 | loop fusion | bytes 655360 | tf_op jit(solution)/shard_map/slice | solution.py:17
  1.7 1.3 %collective-permute-start = (bf16[4,1,160,128]{3,2,1,0:T(8,128)(2,1)S(1)}, bf16[4,1,160,128]{3,2,1,0:T(8,128)(2,1)S(1)}, u32[]{:S(2)}, u32[]{:S(2)}) collective-permute-start(bf16[4,1,160,128]{3,2,1,0:T(8,128)(2,1)S(1)} %get-tuple-element.27), channel_id=1, source_target_pairs={{0,1},{2,3},{4,5},{6,7},{8,9},{10,11},{12,13},{14,15},{16,17},{18,... | collective-permute-start | bytes 491528 | tf_op jit(solution)/shard_map/ppermute | solution.py:20
  3.0 3.0 %collective-permute-start.1 = (bf16[4,1,160,128]{3,2,1,0:T(8,128)(2,1)S(1)}, bf16[4,1,160,128]{3,2,1,0:T(8,128)(2,1)S(1)}, u32[]{:S(2)}, u32[]{:S(2)}) collective-permute-start(bf16[4,1,160,128]{3,2,1,0:T(8,128)(2,1)S(1)} %get-tuple-element.28), channel_id=1, source_target_pairs={{1,0},{3,2},{5,4},{7,6},{9,8},{11,10},{13,12},{15,14},{17,16},{19,... | collective-permute-start | bytes 491528 | tf_op jit(solution)/shard_map/ppermute | solution.py:22
  6.1 1.7 %slice.152 = bf16[2,4,160,128]{3,2,1,0:T(8,128)(2,1)} slice(bf16[4,4,160,128]{3,2,1,0:T(8,128)(2,1)} %param.7), slice={[2:4], [0:4], [0:160], [0:128]} | slice | bytes 655360 | tf_op jit(solution)/shard_map/slice | solution.py:202
  7.8 3.1 %collective-permute-start.5 = (bf16[2,640,128]{2,1,0:T(8,128)(2,1)}, bf16[2,640,128]{2,1,0:T(8,128)(2,1)S(1)}, u32[]{:S(2)}, u32[]{:S(2)}) collective-permute-start(bf16[2,640,128]{2,1,0:T(8,128)(2,1)} %bitcast.22), channel_id=1, source_target_pairs={{0,2},{2,4},{4,6},{6,8},{8,10},{10,12},{12,14},{14,16},{16,18},{18... | collective-permute-start | bytes 983048 | tf_op jit(solution)/shard_map/ppermute | solution.py:32
  10.9 1.0 %slice.148 = bf16[2,4,160,128]{3,2,1,0:T(8,128)(2,1)S(1)} slice(bf16[4,4,160,128]{3,2,1,0:T(8,128)(2,1)} %param.6), slice={[0:2], [0:4], [0:160], [0:128]} | slice | bytes 655360 | tf_op jit(solution)/shard_map/slice | solution.py:201
  11.9 4.0 %collective-permute-start.4 = (bf16[2,640,128]{2,1,0:T(8,128)(2,1)S(1)}, bf16[2,640,128]{2,1,0:T(8,128)(2,1)S(1)}, u32[]{:S(2)}, u32[]{:S(2)}) collective-permute-start(bf16[2,640,128]{2,1,0:T(8,128)(2,1)S(1)} %bitcast.91), channel_id=1, source_target_pairs={{2,0},{4,2},{6,4},{8,6},{10,8},{12,10},{14,12},{16,14},{18,16},{20... | collective-permute-start | bytes 983048 | tf_op jit(solution)/shard_map/ppermute | solution.py:32
  15.9 1.0 %copy.10 = bf16[3,128,128]{1,2,0:T(8,128)(2,1)S(1)} copy(bf16[3,128,128]{2,1,0:T(8,128)(2,1)} %param.9) | data formatting | bytes 196608 | tf_op args[4]
  16.9 1.8 %copy.11 = bf16[3,3,128,128]{2,3,1,0:T(8,128)(2,1)} copy(bf16[3,3,128,128]{3,2,1,0:T(8,128)(2,1)} %param.8) | data formatting | bytes 589824 | tf_op args[3]
  18.8 1.4 %select_maximum_fusion.2 = bf16[4,6,162,128]{3,2,1,0:T(8,128)(2,1)S(1)} fusion(bf16[4,1,160,128]{3,2,1,0:T(8,128)(2,1)S(1)} %collective-permute-done.1, bf16[4,4,160,128]{3,2,1,0:T(8,128)(2,1)} %param.5, bf16[4,1,160,128]{3,2,1,0:T(8,128)(2,1)S(1)} %collective-permute-done), kind=kLoop, calls=%fused_computation.33 | loop fusion | flops 5971968 | bytes 1978368 | tf_op jit(solution)/shard_map/concatenate | solution.py:18
  21.9 1.8 %multiply_convert_fusion = (bf16[2560,128]{1,0:T(8,128)(2,1)S(1)}, f32[2560,128]{1,0:T(8,128)S(1)}) fusion(bf16[2560,1152]{1,0:T(8,128)(2,1)S(1)} %bitcast.99, bf16[1152,128]{1,0:T(8,128)(2,1)S(1)} %bitcast.92), kind=kOutput, calls=%fused_computation.28 | convolution fusion | flops 756613120 | bytes 8159232 | tf_op jit(solution)/shard_map/dot_general | solution.py:196
  23.8 1.9 %collective-permute-start.2 = (bf16[2,640,128]{2,1,0:T(8,128)(2,1)S(1)}, bf16[2,640,128]{2,1,0:T(8,128)(2,1)S(1)}, u32[]{:S(2)}, u32[]{:S(2)}) collective-permute-start(bf16[2,640,128]{2,1,0:T(8,128)(2,1)S(1)} %bitcast.90), channel_id=1, source_target_pairs={{0,2},{2,4},{4,6},{6,8},{8,10},{10,12},{12,14},{14,16},{16,18},{18... | collective-permute-start | bytes 983048 | tf_op jit(solution)/shard_map/ppermute | solution.py:20
  25.7 5.2 %collective-permute-start.3 = (bf16[2,640,128]{2,1,0:T(8,128)(2,1)S(1)}, bf16[2,640,128]{2,1,0:T(8,128)(2,1)S(1)}, u32[]{:S(2)}, u32[]{:S(2)}) collective-permute-start(bf16[2,640,128]{2,1,0:T(8,128)(2,1)S(1)} %bitcast.89), channel_id=1, source_target_pairs={{2,0},{4,2},{6,4},{8,6},{10,8},{12,10},{14,12},{16,14},{18,16},{20... | collective-permute-start | bytes 983048 | tf_op jit(solution)/shard_map/ppermute | solution.py:22
  31.0 0.7 fusion.9
  32.1 0.9 %fusion.5 = bf16[2560,128]{1,0:T(8,128)(2,1)S(1)} fusion(f32[2560,128]{1,0:T(8,128)S(1)} %fusion.9, bf16[384,128]{1,0:T(8,128)(2,1)S(1)} %bitcast.98, bf16[2560,128]{1,0:T(8,128)(2,1)S(1)} %bitcast.77, bf16[2560,128]{1,0:T(8,128)(2,1)S(1)} %bitcast.76, bf16[2560,128]{1,0:T(8,128)(2,1)S(1)} %bitcast.73, f32[2560,128]{1,0:T(8,128)S(1)} %get-tuple-element.30), kind=kOutput, calls=%fused_computation.9 | convolution fusion | flops 260833280 | bytes 5341184 | tf_op jit(solution)/shard_map/dot_general | solution.py:221
  33.0 0.8 fusion.39
  33.8 1.3 %collective-permute-start.6 = (bf16[4,1,160,128]{3,2,1,0:T(8,128)(2,1)}, bf16[4,1,160,128]{3,2,1,0:T(8,128)(2,1)S(1)}, u32[]{:S(2)}, u32[]{:S(2)}) collective-permute-start(bf16[4,1,160,128]{3,2,1,0:T(8,128)(2,1)} %get-tuple-element.21), channel_id=1, source_target_pairs={{0,1},{2,3},{4,5},{6,7},{8,9},{10,11},{12,13},{14,15},{16,17},{18,... | collective-permute-start | bytes 491528 | tf_op jit(solution)/shard_map/ppermute | solution.py:20
  35.1 3.7 %collective-permute-start.7 = (bf16[4,1,160,128]{3,2,1,0:T(8,128)(2,1)}, bf16[4,1,160,128]{3,2,1,0:T(8,128)(2,1)}, u32[]{:S(2)}, u32[]{:S(2)}) collective-permute-start(bf16[4,1,160,128]{3,2,1,0:T(8,128)(2,1)} %get-tuple-element.22), channel_id=1, source_target_pairs={{1,0},{3,2},{5,4},{7,6},{9,8},{11,10},{13,12},{15,14},{17,16},{19,... | collective-permute-start | bytes 491528 | tf_op jit(solution)/shard_map/ppermute | solution.py:22
  38.8 1.7 %fusion.42 = f32[1152,128]{1,0:T(8,128)S(1)} fusion(bf16[2560,1152]{1,0:T(8,128)(2,1)S(1)} %bitcast.100, bf16[2560,128]{1,0:T(8,128)(2,1)S(1)} %fusion.5), kind=kOutput, calls=%fused_computation.86 | convolution fusion | flops 754974720 | bytes 7143424 | tf_op jit(solution)/shard_map/dot_general | solution.py:60
  40.6 1.6 %collective-permute-done.3 = bf16[2,640,128]{2,1,0:T(8,128)(2,1)S(1)} collective-permute-done((bf16[2,640,128]{2,1,0:T(8,128)(2,1)S(1)}, bf16[2,640,128]{2,1,0:T(8,128)(2,1)S(1)}, u32[]{:S(2)}, u32[]{:S(2)}) %collective-permute-start.3) | collective-permute-done | bytes 327712 | tf_op jit(solution)/shard_map/ppermute | solution.py:22
  42.4 0.7 fusion.21
  43.1 0.7 convolution_add_fusion.4
  43.9 0.9 %pad_maximum_fusion.2.x_ref = f32[1536,128]{1,0:T(8,128)} fusion(f32[384,128]{1,0:T(8,128)S(1)} %convolution_add_fusion.4, f32[1152,128]{1,0:T(8,128)S(1)} %fusion.42), kind=kLoop, calls=%fused_computation.45 | loop fusion | flops 196608 | bytes 1572864 | tf_op jit(solution)/shard_map/concatenate | solution.py:236
  44.9 30.8 %shard_map.92 = f32[1536,128]{1,0:T(8,128)} custom-call(f32[1536,128]{1,0:T(8,128)} %pad_maximum_fusion.2.x_ref), custom_call_target="tpu_custom_call" | custom-call | tf_op jit(solution)/shard_map/pallas_call | solution.py:167
  75.6 1.6 %slice.167 = f32[384,128]{1,0:T(8,128)} slice(f32[1536,128]{1,0:T(8,128)} %shard_map.92), slice={[1152:1536], [0:128]} | slice | bytes 393216 | tf_op jit(solution)/shard_map/slice | solution.py:238
  77.3 2.0 %slice.166 = f32[1152,128]{1,0:T(8,128)} slice(f32[1536,128]{1,0:T(8,128)} %shard_map.92), slice={[0:1152], [0:128]} | slice | bytes 1179648 | tf_op jit(solution)/shard_map/slice | solution.py:237
  79.3 2.8 %fusion.3 = bf16[2560,128]{1,0:T(8,128)(2,1)} fusion(bf16[384,128]{1,0:T(8,128)(2,1)S(1)} %bitcast.95, bf16[2560,128]{1,0:T(8,128)(2,1)S(1)} %bitcast.54, bf16[2560,128]{1,0:T(8,128)(2,1)S(1)} %get-tuple-element.29, bf16[2560,128]{1,0:T(8,128)(2,1)} %bitcast.87, bf16[2560,128]{1,0:T(8,128)(2,1)} %bitcast.85), kind=kOutput, calls=%fused_computation.7 | convolution fusion | flops 258539520 | bytes 3375104 | tf_op jit(solution)/shard_map/dot_general | solution.py:212
  82.1 1.5 %fusion.2 = bf16[2560,128]{1,0:T(8,128)(2,1)} fusion(bf16[384,128]{1,0:T(8,128)(2,1)S(1)} %bitcast.96, bf16[2560,128]{1,0:T(8,128)(2,1)S(1)} %bitcast.55, bf16[2560,128]{1,0:T(8,128)(2,1)S(1)} %get-tuple-element.29, bf16[2560,128]{1,0:T(8,128)(2,1)S(1)} %bitcast.81, bf16[2560,128]{1,0:T(8,128)(2,1)S(1)} %bitcast.83), kind=kOutput, calls=%fused_computation.6 | convolution fusion | flops 258539520 | bytes 3375104 | tf_op jit(solution)/shard_map/dot_general | solution.py:207
  83.6 1.2 %select_maximum_fusion = bf16[4,6,162,128]{3,2,1,0:T(8,128)(2,1)S(1)} fusion(bf16[4,1,160,128]{3,2,1,0:T(8,128)(2,1)} %collective-permute-done.7, bf16[4,4,160,128]{3,2,1,0:T(8,128)(2,1)S(1)} %bitcast.57, bf16[4,1,160,128]{3,2,1,0:T(8,128)(2,1)S(1)} %collective-permute-done.6), kind=kLoop, calls=%fused_computation.31 | loop fusion | flops 5971968 | bytes 1978368 | tf_op jit(solution)/shard_map/concatenate | solution.py:18
  84.8 0.6 fusion.38
  85.6 1.0 %pad_maximum_fusion.3 = (bf16[4,4,160,128]{3,2,1,0:T(8,128)(2,1)S(1)}, bf16[4,4,160,128]{3,2,1,0:T(8,128)(2,1)S(1)}) fusion(bf16[4,4,160,128]{3,2,1,0:T(8,128)(2,1)S(1)} %bitcast.58, bf16[4,1,160,128]{3,2,1,0:T(8,128)(2,1)S(1)} %collective-permute-done.6, bf16[4,1,160,128]{3,2,1,0:T(8,128)(2,1)} %collective-permute-done.7), kind=kLoop, calls=%fused_computation.50 | loop fusion | flops 655360 | bytes 2293760 | tf_op jit(solution)/shard_map/concatenate | solution.py:18
  87.9 2.6 %fusion.4 = bf16[2560,128]{1,0:T(8,128)(2,1)} fusion(bf16[2560,1152]{1,0:T(8,128)(2,1)S(1)} %constant_dynamic-update-slice_fusion.1, bf16[1152,128]{1,0:T(8,128)(2,1)S(1)} %bitcast.93, bf16[2560,128]{1,0:T(8,128)(2,1)S(1)} %bitcast.75, bf16[2560,128]{1,0:T(8,128)(2,1)S(1)} %bitcast.71), kind=kOutput, calls=%fused_computation.8 | convolution fusion | flops 756613120 | bytes 8159232 | tf_op jit(solution)/shard_map/dot_general | solution.py:231
  (53 shorter events, 3.9 us)
Async XLA Ops:
  0.6 19.6 %copy-start = (bf16[4,4,160,128]{3,2,1,0:T(8,128)(2,1)S(1)}, bf16[4,4,160,128]{3,2,1,0:T(8,128)(2,1)}, u32[]{:S(2)}) copy-start(bf16[4,4,160,128]{3,2,1,0:T(8,128)(2,1)} %param.5) | copy-start | bytes 1966084
  1.7 17.0 %collective-permute-start = (bf16[4,1,160,128]{3,2,1,0:T(8,128)(2,1)S(1)}, bf16[4,1,160,128]{3,2,1,0:T(8,128)(2,1)S(1)}, u32[]{:S(2)}, u32[]{:S(2)}) collective-permute-start(bf16[4,1,160,128]{3,2,1,0:T(8,128)(2,1)S(1)} %get-tuple-element.27), channel_id=1, source_target_pairs={{0,1},{2,3},{4,5},{6,7},{8,9},{10,11},{12,13},{14,15},{16,17},{18,... | collective-permute-start | bytes 491528 | tf_op jit(solution)/shard_map/ppermute | solution.py:20
  3.0 15.7 %collective-permute-start.1 = (bf16[4,1,160,128]{3,2,1,0:T(8,128)(2,1)S(1)}, bf16[4,1,160,128]{3,2,1,0:T(8,128)(2,1)S(1)}, u32[]{:S(2)}, u32[]{:S(2)}) collective-permute-start(bf16[4,1,160,128]{3,2,1,0:T(8,128)(2,1)S(1)} %get-tuple-element.28), channel_id=1, source_target_pairs={{1,0},{3,2},{5,4},{7,6},{9,8},{11,10},{13,12},{15,14},{17,16},{19,... | collective-permute-start | bytes 491528 | tf_op jit(solution)/shard_map/ppermute | solution.py:22
  7.8 23.9 %collective-permute-start.5 = (bf16[2,640,128]{2,1,0:T(8,128)(2,1)}, bf16[2,640,128]{2,1,0:T(8,128)(2,1)S(1)}, u32[]{:S(2)}, u32[]{:S(2)}) collective-permute-start(bf16[2,640,128]{2,1,0:T(8,128)(2,1)} %bitcast.22), channel_id=1, source_target_pairs={{0,2},{2,4},{4,6},{6,8},{8,10},{10,12},{12,14},{14,16},{16,18},{18... | collective-permute-start | bytes 983048 | tf_op jit(solution)/shard_map/ppermute | solution.py:32
  11.9 19.0 %collective-permute-start.4 = (bf16[2,640,128]{2,1,0:T(8,128)(2,1)S(1)}, bf16[2,640,128]{2,1,0:T(8,128)(2,1)S(1)}, u32[]{:S(2)}, u32[]{:S(2)}) collective-permute-start(bf16[2,640,128]{2,1,0:T(8,128)(2,1)S(1)} %bitcast.91), channel_id=1, source_target_pairs={{2,0},{4,2},{6,4},{8,6},{10,8},{12,10},{14,12},{16,14},{18,16},{20... | collective-permute-start | bytes 983048 | tf_op jit(solution)/shard_map/ppermute | solution.py:32
  20.7 1.2 %copy-start.9 = (bf16[3,3,128,128]{3,2,1,0:T(8,128)(2,1)S(1)}, bf16[3,3,128,128]{3,2,1,0:T(8,128)(2,1)}, u32[]{:S(2)}) copy-start(bf16[3,3,128,128]{3,2,1,0:T(8,128)(2,1)} %param.8) | copy-start | bytes 884740
  21.9 9.0 %copy-start.1 = (bf16[4,4,160,128]{3,2,1,0:T(8,128)(2,1)S(1)}, bf16[4,4,160,128]{3,2,1,0:T(8,128)(2,1)}, u32[]{:S(2)}) copy-start(bf16[4,4,160,128]{3,2,1,0:T(8,128)(2,1)} %param.6) | copy-start | bytes 1966084
  23.8 16.7 %collective-permute-start.2 = (bf16[2,640,128]{2,1,0:T(8,128)(2,1)S(1)}, bf16[2,640,128]{2,1,0:T(8,128)(2,1)S(1)}, u32[]{:S(2)}, u32[]{:S(2)}) collective-permute-start(bf16[2,640,128]{2,1,0:T(8,128)(2,1)S(1)} %bitcast.90), channel_id=1, source_target_pairs={{0,2},{2,4},{4,6},{6,8},{8,10},{10,12},{12,14},{14,16},{16,18},{18... | collective-permute-start | bytes 983048 | tf_op jit(solution)/shard_map/ppermute | solution.py:20
  25.7 16.4 %collective-permute-start.3 = (bf16[2,640,128]{2,1,0:T(8,128)(2,1)S(1)}, bf16[2,640,128]{2,1,0:T(8,128)(2,1)S(1)}, u32[]{:S(2)}, u32[]{:S(2)}) collective-permute-start(bf16[2,640,128]{2,1,0:T(8,128)(2,1)S(1)} %bitcast.89), channel_id=1, source_target_pairs={{2,0},{4,2},{6,4},{8,6},{10,8},{12,10},{14,12},{16,14},{18,16},{20... | collective-permute-start | bytes 983048 | tf_op jit(solution)/shard_map/ppermute | solution.py:22
  30.9 1.1 %copy-start.2 = (bf16[4,4,160,128]{3,2,1,0:T(8,128)(2,1)S(1)}, bf16[4,4,160,128]{3,2,1,0:T(8,128)(2,1)}, u32[]{:S(2)}) copy-start(bf16[4,4,160,128]{3,2,1,0:T(8,128)(2,1)} %param.7) | copy-start | bytes 1966084
  33.8 49.8 %collective-permute-start.6 = (bf16[4,1,160,128]{3,2,1,0:T(8,128)(2,1)}, bf16[4,1,160,128]{3,2,1,0:T(8,128)(2,1)S(1)}, u32[]{:S(2)}, u32[]{:S(2)}) collective-permute-start(bf16[4,1,160,128]{3,2,1,0:T(8,128)(2,1)} %get-tuple-element.21), channel_id=1, source_target_pairs={{0,1},{2,3},{4,5},{6,7},{8,9},{10,11},{12,13},{14,15},{16,17},{18,... | collective-permute-start | bytes 491528 | tf_op jit(solution)/shard_map/ppermute | solution.py:20
  35.1 48.5 %collective-permute-start.7 = (bf16[4,1,160,128]{3,2,1,0:T(8,128)(2,1)}, bf16[4,1,160,128]{3,2,1,0:T(8,128)(2,1)}, u32[]{:S(2)}, u32[]{:S(2)}) collective-permute-start(bf16[4,1,160,128]{3,2,1,0:T(8,128)(2,1)} %get-tuple-element.22), channel_id=1, source_target_pairs={{1,0},{3,2},{5,4},{7,6},{9,8},{11,10},{13,12},{15,14},{17,16},{19,... | collective-permute-start | bytes 491528 | tf_op jit(solution)/shard_map/ppermute | solution.py:22
  42.4 1.5 %copy-start.3 = (bf16[4,640,128]{2,1,0:T(8,128)(2,1)}, bf16[4,640,128]{2,1,0:T(8,128)(2,1)S(1)}, u32[]{:S(2)}) copy-start(bf16[4,640,128]{2,1,0:T(8,128)(2,1)S(1)} %get-tuple-element.23) | copy-start | bytes 1966084
  42.4 1.5 %copy-start.5 = (bf16[4,640,128]{2,1,0:T(8,128)(2,1)}, bf16[4,640,128]{2,1,0:T(8,128)(2,1)S(1)}, u32[]{:S(2)}) copy-start(bf16[4,640,128]{2,1,0:T(8,128)(2,1)S(1)} %get-tuple-element.24) | copy-start | bytes 1966084
  42.4 1.5 %copy-start.7 = (bf16[4,640,128]{2,1,0:T(8,128)(2,1)}, bf16[4,640,128]{2,1,0:T(8,128)(2,1)S(1)}, u32[]{:S(2)}) copy-start(bf16[4,640,128]{2,1,0:T(8,128)(2,1)S(1)} %get-tuple-element.15) | copy-start | bytes 1966084
  42.4 1.5 %copy-start.8 = (bf16[4,640,128]{2,1,0:T(8,128)(2,1)}, bf16[4,640,128]{2,1,0:T(8,128)(2,1)S(1)}, u32[]{:S(2)}) copy-start(bf16[4,640,128]{2,1,0:T(8,128)(2,1)S(1)} %get-tuple-element.16) | copy-start | bytes 1966084
  43.9 35.4 %copy-start.11 = (bf16[3,128,128]{2,1,0:T(8,128)(2,1)S(1)}, bf16[3,128,128]{2,1,0:T(8,128)(2,1)}, u32[]{:S(2)}) copy-start(bf16[3,128,128]{2,1,0:T(8,128)(2,1)} %param.9) | copy-start | bytes 294916
  77.3 4.8 %copy-start.4 = (bf16[4,640,128]{2,1,0:T(8,128)(2,1)S(1)}, bf16[4,640,128]{2,1,0:T(8,128)(2,1)}, u32[]{:S(2)}) copy-start(bf16[4,640,128]{2,1,0:T(8,128)(2,1)} %copy-done.3) | copy-start | bytes 1966084
  77.3 4.8 %copy-start.6 = (bf16[4,640,128]{2,1,0:T(8,128)(2,1)S(1)}, bf16[4,640,128]{2,1,0:T(8,128)(2,1)}, u32[]{:S(2)}) copy-start(bf16[4,640,128]{2,1,0:T(8,128)(2,1)} %copy-done.5) | copy-start | bytes 1966084
  86.9 1.0 %copy-start.10 = (bf16[3,3,128,128]{2,3,1,0:T(8,128)(2,1)S(1)}, bf16[3,3,128,128]{2,3,1,0:T(8,128)(2,1)}, u32[]{:S(2)}) copy-start(bf16[3,3,128,128]{2,3,1,0:T(8,128)(2,1)} %copy.11) | copy-start | bytes 884740

commit v2 on v0

v2 whole, which is shorter than its diff:
```python
import functools
import math

import jax
import jax.numpy as jnp
from jax import lax
from jax.experimental import pallas as pl
from jax.experimental.pallas import tpu as pltpu
from jax.sharding import PartitionSpec as P

MESH = pl.DeviceIdType.MESH


def at(start, size):
    return pl.ds(pl.multiple_of(start, 8), size)


def each(count, act):
    def step(index, carry):
        act(index)
        return carry

    lax.fori_loop(1, count, step, 0)


def frames(first, last, act):
    def step(index, carry):
        act(index)
        return carry

    lax.fori_loop(first, last, step, 0)


def columns(rows, width, channels):
    place = lax.broadcasted_iota(jnp.int32, (rows // width, width, channels), 1)
    return place.reshape(rows, channels)


def before(value, place):
    return jnp.where(place == 0, 0.0, pltpu.roll(value, 1, 0))


def after(value, place, width):
    return jnp.where(place == width - 1, 0.0, pltpu.roll(value, value.shape[0] - 1, 0))


def spread(value, place, width):
    kind = jnp.bfloat16
    return jnp.concatenate(
        [after(value, place, width).astype(kind), value.astype(kind), before(value, place).astype(kind)],
        axis=1,
    )


def flat(value):
    return value.reshape(-1, value.shape[-1])


def across(left, right):
    return lax.dot_general(
        left, right, (((1,), (1,)), ((), ())), preferred_element_type=jnp.float32
    )


def contract(left, right):
    return lax.dot_general(
        left, right, (((0,), (0,)), ((), ())), preferred_element_type=jnp.float32
    )


def kernel(
    tiles,
    shards,
    scale,
    latent_ref,
    fwd_ref,
    rev_ref,
    space_ref,
    time_ref,
    out_f_ref,
    out_r_ref,
    grad_in_ref,
    grad_s_ref,
    grad_t_ref,
    cells,
    cot_f,
    cot_r,
    acts,
    pre,
    wide,
    rim_out,
    rim_in,
    space_fwd,
    space_back,
    time_back,
    sums,
    pair_in,
    mid,
    shard_in,
    total,
    load_sem,
    send_sem,
    recv_sem,
):
    tile, shard = lax.axis_index("tile"), lax.axis_index("tm")
    count, height, width, channels = latent_ref.shape
    plane = height * width
    taps = 3

    def tile_peer(step):
        return {"tile": lax.rem(tile + step, tiles)}

    def shard_peer(step):
        return {"tm": lax.rem(shard + step, shards)}

    barrier = pltpu.get_barrier_semaphore()

    def greet(peer):
        pl.semaphore_signal(barrier, inc=1, device_id=peer, device_id_type=MESH)

    each(tiles, lambda step: greet(tile_peer(step)))
    each(shards, lambda step: greet(shard_peer(step)))

    loads = [
        pltpu.make_async_copy(latent_ref, cells.at[:, pl.ds(1, height)], load_sem.at[0]),
        pltpu.make_async_copy(fwd_ref, cot_f.at[pl.ds(0, count)], load_sem.at[1]),
        pltpu.make_async_copy(rev_ref, cot_r.at[pl.ds(2, count)], load_sem.at[2]),
    ]
    for load in loads:
        load.start()

    has_next_tile, has_last_tile = tile < tiles - 1, tile > 0
    has_next_shard, has_last_shard = shard < shards - 1, shard > 0

    def remote(src, dst, index, peer):
        return pltpu.make_async_remote_copy(
            src_ref=src,
            dst_ref=dst,
            send_sem=send_sem.at[index],
            recv_sem=recv_sem.at[index],
            device_id=peer,
            device_id_type=MESH,
        )

    next_tile, last_tile = tile_peer(1), tile_peer(tiles - 1)
    next_shard, last_shard = shard_peer(1), shard_peer(shards - 1)
    moves = [
        (latent_ref.at[:, height - 1], cells.at[:, 0], next_tile, has_next_tile, has_last_tile),
        (latent_ref.at[:, 0], cells.at[:, height + 1], last_tile, has_last_tile, has_next_tile),
        (
            fwd_ref.at[pl.ds(0, 2)],
            cot_f.at[pl.ds(count, 2)],
            last_shard,
            has_last_shard,
            has_next_shard,
        ),
        (
            rev_ref.at[pl.ds(count - 2, 2)],
            cot_r.at[pl.ds(0, 2)],
            next_shard,
            has_next_shard,
            has_last_shard,
        ),
        (
            acts.at[pl.ds(count, 2)],
            acts.at[pl.ds(0, 2)],
            next_shard,
            has_next_shard,
            has_last_shard,
        ),
        (
            acts.at[pl.ds(2, 2)],
            acts.at[pl.ds(count + 2, 2)],
            last_shard,
            has_last_shard,
            has_next_shard,
        ),
        (rim_out.at[1], rim_in.at[0], next_tile, has_next_tile, has_last_tile),
        (rim_out.at[0], rim_in.at[1], last_tile, has_last_tile, has_next_tile),
    ]
    copies = [remote(src, dst, index, peer) for index, (src, dst, peer, _, _) in enumerate(moves)]

    def launch(index):
        pl.when(moves[index][3])(copies[index].start)

    def arrive(index):
        pl.when(moves[index][4])(copies[index].wait_recv)

    def leave(index):
        pl.when(moves[index][3])(copies[index].wait_send)

    for index in range(8):
        if index < 6:
            target = moves[index][1]

            @pl.when(jnp.logical_not(moves[index][4]))
            def _(target=target):
                target[...] = jnp.zeros(target.shape, target.dtype)

        else:
            target = rim_in.at[index - 6]

            @pl.when(jnp.logical_not(moves[index][4]))
            def _(target=target):
                target[...] = jnp.zeros(target.shape, target.dtype)

    sums[...] = jnp.zeros_like(sums)
    for row in range(taps):
        time_back[:, row * channels : (row + 1) * channels] = time_ref[
            row * channels : (row + 1) * channels, :
        ]
        time_back[:, (taps + row) * channels : (taps + row + 1) * channels] = time_ref[
            row * channels : (row + 1) * channels, :
        ]
        for col in range(taps):
            index = row * taps + col
            weight = space_ref[index * channels : (index + 1) * channels, :]
            space_fwd[
                row * channels : (row + 1) * channels, col * channels : (col + 1) * channels
            ] = weight
            space_back[:, index * channels : (index + 1) * channels] = weight

    pl.semaphore_wait(barrier, tiles + shards - 2)
    for index in range(4):
        launch(index)
    place = columns(plane, width, channels)

    def window(frame):
        return jnp.concatenate(
            [flat(cells[frame, pl.ds(row, height)]) for row in range(taps)], axis=1
        )

    loads[0].wait()
    arrive(0)
    arrive(1)

    def convolve(frame):
        parts = jnp.dot(window(frame), space_fwd[...], preferred_element_type=jnp.float32)
        value = (
            before(parts[:, :channels], place)
            + parts[:, channels : 2 * channels]
            + after(parts[:, 2 * channels :], place, width)
        )
        pre[frame] = value
        act = value / (1.0 + jnp.exp(-value))
        acts[frame + 2] = act.astype(jnp.bfloat16).reshape(height, width, channels)

    frames(0, count, convolve)
    launch(4)
    launch(5)

    loads[1].wait()
    loads[2].wait()
    arrive(2)
    arrive(3)

    def backward(frame):
        joined = jnp.concatenate(
            [flat(cot_f[frame + lag]) for lag in range(taps)]
            + [flat(cot_r[frame + 2 - lag]) for lag in range(taps)],
            axis=1,
        )
        grad_act = across(joined, time_back[...])
        value = pre[frame]
        gate = 1.0 / (1.0 + jnp.exp(-value))
        grad = grad_act * gate * (1.0 + value * (1.0 - gate))
        grad = grad.astype(jnp.bfloat16).astype(jnp.float32)
        shifted = spread(grad, place, width)
        wide[frame, pl.ds(1, height)] = shifted.reshape(height, width, taps * channels)
        rounded = grad.astype(jnp.bfloat16)
        rim_out[0, frame] = rounded[:width]
        rim_out[1, frame] = rounded[plane - width :]
        lags = contract(flat(acts[frame + 2]), joined)
        for lag in range(taps):
            row = (taps * taps + lag) * channels
            sums[row : row + channels, :] += (
                lags[:, lag * channels : (lag + 1) * channels]
                + lags[:, (taps + lag) * channels : (taps + lag + 1) * channels]
            )
        part = contract(window(frame), shifted)
        for row in range(taps):
            for col in range(taps):
                start = (row * taps + col) * channels
                sums[start : start + channels, :] += part[
                    row * channels : (row + 1) * channels, col * channels : (col + 1) * channels
                ]

    frames(0, count, backward)
    launch(6)
    launch(7)

    half = sums.shape[0] // tiles
    chunk = half // shards

    def settle(phase, ref):
        pltpu.make_async_copy(ref, ref, send_sem.at[phase]).wait()
        pltpu.make_async_copy(ref, ref, recv_sem.at[phase]).wait()

    def rows_to(step):
        return lax.rem(tile + step, tiles) * half

    each(
        tiles,
        lambda step: remote(
            sums.at[at(rows_to(step), half)], pair_in.at[step - 1], 8, tile_peer(step)
        ).start(),
    )

    def outputs(frame):
        base = flat(cells[frame, pl.ds(1, height)]).astype(jnp.float32)
        causal = jnp.concatenate([flat(acts[frame + 2 - lag]) for lag in range(taps)], axis=1)
        anticausal = jnp.concatenate([flat(acts[frame + 2 + lag]) for lag in range(taps)], axis=1)
        for joined, ref in ((causal, out_f_ref), (anticausal, out_r_ref)):
            value = base + jnp.dot(joined, time_ref[...], preferred_element_type=jnp.float32)
            ref[frame] = value.astype(jnp.bfloat16).reshape(height, width, channels)

    def input_grads(frame):
        joined = jnp.concatenate(
            [flat(wide[frame, pl.ds(2 - row, height)]) for row in range(taps)], axis=1
        )
        value = flat(cot_f[frame]).astype(jnp.float32) + flat(cot_r[frame + 2]).astype(jnp.float32)
        value = value + across(joined, space_back[...])
        grad_in_ref[frame] = value.astype(jnp.bfloat16).reshape(height, width, channels)

    settle(8, pair_in)
    own_half = sums[at(tile * half, half), :]
    for index in range(tiles - 1):
        own_half = own_half + pair_in[index]
    mid[...] = own_half
    each(
        shards,
        lambda step: remote(
            mid.at[at(lax.rem(shard + step, shards) * chunk, chunk)],
            shard_in.at[step - 1],
            9,
            shard_peer(step),
        ).start(),
    )
    arrive(4)
    arrive(5)
    frames(0, count, outputs)
    settle(9, shard_in)
    part = lax.fori_loop(
        0,
        shards - 1,
        lambda index, value: value + shard_in[index],
        mid[at(shard * chunk, chunk), :],
    )
    own = at(tile * half + shard * chunk, chunk)
    total[own, :] = part * scale
    each(
        shards,
        lambda step: remote(total.at[own], total.at[own], 10, shard_peer(step)).start(),
    )
    arrive(6)
    arrive(7)
    edge = columns(count * width, width, channels)
    for side, row in ((0, 0), (1, height + 1)):
        rim = spread(flat(rim_in[side]).astype(jnp.float32), edge, width)
        wide[:, row] = rim.reshape(count, width, taps * channels)
    frames(0, count, input_grads)
    settle(10, total.at[pl.ds(0, (shards - 1) * chunk)])
    mine = at(tile * half, half)
    each(
        tiles,
        lambda step: remote(total.at[mine], total.at[mine], 11, tile_peer(step)).start(),
    )
    for index in range(8):
        leave(index)
    settle(11, total.at[pl.ds(0, (tiles - 1) * half)])
    split = taps * taps * channels
    grad_s_ref[...] = total[:split, :]
    grad_t_ref[...] = total[split : split + taps * channels, :]


def body(latent, cot_forward, cot_reverse, spatial_weight, temporal_weight):
    tiles, shards = lax.axis_size("tile"), lax.axis_size("tm")
    count, height, width, channels = latent.shape
    positions = count * height * width * shards * tiles
    scale = 1.0 / math.sqrt(positions)
    rows = 12 * channels
    unit = 8 * tiles * shards
    padded = -(-rows // unit) * unit
    half = padded // tiles
    chunk = half // shards
    kind = jnp.bfloat16
    vmem = pl.BlockSpec(memory_space=pltpu.VMEM)
    hbm = pl.BlockSpec(memory_space=pl.ANY)
    out_f, out_r, grad_in, grad_s, grad_t = pl.pallas_call(
        functools.partial(kernel, tiles, shards, scale),
        out_shape=(
            jax.ShapeDtypeStruct(latent.shape, kind),
            jax.ShapeDtypeStruct(latent.shape, kind),
            jax.ShapeDtypeStruct(latent.shape, kind),
            jax.ShapeDtypeStruct((9 * channels, channels), jnp.float32),
            jax.ShapeDtypeStruct((3 * channels, channels), jnp.float32),
        ),
        in_specs=[hbm, hbm, hbm, vmem, vmem],
        out_specs=(vmem, vmem, vmem, vmem, vmem),
        scratch_shapes=[
            pltpu.VMEM((count, height + 2, width, channels), kind),
            pltpu.VMEM((count + 2, height, width, channels), kind),
            pltpu.VMEM((count + 2, height, width, channels), kind),
            pltpu.VMEM((count + 4, height, width, channels), kind),
            pltpu.VMEM((count, height * width, channels), jnp.float32),
            pltpu.VMEM((count, height + 2, width, 3 * channels), kind),
            pltpu.VMEM((2, count, width, channels), kind),
            pltpu.VMEM((2, count, width, channels), kind),
            pltpu.VMEM((3 * channels, 3 * channels), kind),
            pltpu.VMEM((channels, 9 * channels), kind),
            pltpu.VMEM((channels, 6 * channels), kind),
            pltpu.VMEM((padded, channels), jnp.float32),
            pltpu.VMEM((tiles - 1, half, channels), jnp.float32),
            pltpu.VMEM((half, channels), jnp.float32),
            pltpu.VMEM((shards - 1, chunk, channels), jnp.float32),
            pltpu.VMEM((padded, channels), jnp.float32),
            pltpu.SemaphoreType.DMA((3,)),
            pltpu.SemaphoreType.DMA((12,)),
            pltpu.SemaphoreType.DMA((12,)),
        ],
        compiler_params=pltpu.CompilerParams(collective_id=0, has_side_effects=True),
    )(
        latent,
        cot_forward,
        cot_reverse,
        spatial_weight.reshape(9 * channels, channels),
        temporal_weight.reshape(3 * channels, channels),
    )
    return (
        out_f,
        out_r,
        grad_in,
        grad_s.reshape(spatial_weight.shape),
        grad_t.reshape(temporal_weight.shape),
    )


def solution(mesh):
    placed = (
        P("tm", "tile", None, None),
        P("tm", "tile", None, None),
        P("tm", "tile", None, None),
        P(),
        P(),
    )
    return jax.shard_map(
        body,
        mesh=mesh,
        in_specs=placed,
        out_specs=(
            P("tm", "tile", None, None),
            P("tm", "tile", None, None),
            P("tm", "tile", None, None),
            P(),
            P(),
        ),
        check_vma=False,
    )
```

time: 197 us -> 66.4 us (0.34)
  waiting for transfers between devices: 122 us -> 0 us
  Pallas kernels: 0 us -> 58.2 us
  starting transfers between devices: 18.6 us -> 0 us
  matrix products: 16.4 us -> 0 us
  between operations: 14.4 us -> 0.65 us
  local copies, waits for them, and re-layouts: 19.6 us -> 6.46 us
  other arithmetic: 6.05 us -> 0 us
    psum x1 -> x0, waiting for transfers between devices: 120 us -> none  [body(): grad_space, grad_temp = lax.psum((grad_space, grad_temp), ('tm', 'tile'))]
    pallas_call x0 -> x1, Pallas kernels: none -> 58.2 us  [body(): pl.pallas_call(functools.partial(kernel, tiles, shards, scale), out_shape...]
    ppermute x8 -> x0, starting transfers between devices: 18.6 us -> none  [the longest x3 9 us: extended_2(): lax.ppermute(tail, axis, [(i, (i + 1) % count) for i in range(ends)])]
    dot_general x9 -> x0, matrix products: 16.4 us -> none  [the longest x1 5.35 us: body(): jnp.dot(grad_patches, flipped_flat, preferred_element_type=jnp.float32)]
    unnamed x48 -> x13, local copies, waits for them, and re-layouts: 13.9 us -> 6.46 us
    slice x6 -> x0, local copies, waits for them, and re-layouts: 4.5 us -> none  [the longest x1 1.36 us: spatial_rows(): padded[:, row_from:row_from + height, col_from:col_from + width_cells, :]]
    mul x2 -> x0, other arithmetic: 3.55 us -> none  [the longest x1 1.93 us: body(): grad_spatial = (grad_space * grad_scale).reshape(3, 3, channels, channels)]
    concatenate x6 -> x0, other arithmetic: 2.19 us -> none  [the longest x4 2.02 us: extended_2(): jnp.concatenate([lax.ppermute(tail, axis, [(i, (i + 1) % count) for i in...]
  transfers between devices with their start and end apart: 9 -> 0, of which waited for: 3 -> 0; matrix products, arithmetic and copies ran while one was open for 17% -> 0% of each run, Pallas kernels for 0% -> 0%
where the time goes in v2:
time: 66.4 us; the launch traced here: 65.3 us
  Pallas kernels  58.2 us (88%)
  local copies, waits for them, and re-layouts  6.46 us (10%)
    pallas_call x1, Pallas kernels, body(): pl.pallas_call(functools.partial(kernel, tiles, shards, scale), out_shape...  58.2 us
    unnamed x13, local copies, waits for them, and re-layouts  6.46 us

profile of v2, /device:TPU:0, one launch (start us, length us, event | category | flops | bytes accessed | tf_op | source)
XLA Modules:
  0.0 65.3 jit_solution(8623575314272619501)
XLA Ops:
  0.6 58.2 %shard_map.92 = (bf16[4,4,160,128]{3,2,1,0:T(8,128)(2,1)}, bf16[4,4,160,128]{3,2,1,0:T(8,128)(2,1)}, bf16[4,4,160,128]{3,2,1,0:T(8,128)(2,1)}, f32[1152,128]{1,0:T(8,128)}, f32[384,128]{1,0:T(8,128)}) custom-call(bf16[4,4,160,128]{3,2,1,0:T(8,128)(2,1)} %latent_ref.1, bf16[4,4,160,128]{3,2,1,0:T(8,128)(2,1)} %fwd_ref.1, bf16[4,4,160,128]{3,2,1,0:T(8,128)(2,1)} %rev_ref.1, ...), custom_call_target="tpu_custom_call" | custom-call | tf_op jit(solution)/shard_map/pallas_call | solution.py:389
  58.8 0.0 copy-start.1
  58.8 2.0 %copy.15 = bf16[4,4,160,128]{3,2,1,0:T(8,128)(2,1)} copy(bf16[4,4,160,128]{3,2,1,0:T(8,128)(2,1)} %get-tuple-element.20) | data formatting | bytes 1310720
  60.9 0.0 copy-done.1
  60.9 0.0 copy-start
  60.9 0.8 %copy.16 = bf16[4,4,160,128]{3,2,1,0:T(8,128)(2,1)} copy(bf16[4,4,160,128]{3,2,1,0:T(8,128)(2,1)S(1)} %copy-done.1) | data formatting | bytes 1310720
  61.7 0.5 copy-done
  62.2 0.0 copy-start.2
  62.2 0.8 %copy.17 = bf16[4,4,160,128]{3,2,1,0:T(8,128)(2,1)} copy(bf16[4,4,160,128]{3,2,1,0:T(8,128)(2,1)S(1)} %copy-done) | data formatting | bytes 1310720
  63.0 0.5 copy-done.2
  63.5 0.0 copy-start.3
  63.5 0.8 %copy.18 = f32[3,3,128,128]{3,2,1,0:T(8,128)} copy(f32[3,3,128,128]{3,2,1,0:T(8,128)S(1)} %bitcast.4) | data formatting | bytes 1179648
  64.3 0.3 copy-done.3
  64.6 0.7 %copy.19 = f32[3,128,128]{2,1,0:T(8,128)} copy(f32[3,128,128]{2,1,0:T(8,128)S(1)} %bitcast.6) | data formatting | bytes 393216
Async XLA Ops:
  58.8 2.1 %copy-start.1 = (bf16[4,4,160,128]{3,2,1,0:T(8,128)(2,1)S(1)}, bf16[4,4,160,128]{3,2,1,0:T(8,128)(2,1)}, u32[]{:S(2)}) copy-start(bf16[4,4,160,128]{3,2,1,0:T(8,128)(2,1)} %get-tuple-element.21) | copy-start | bytes 1966084
  60.9 1.3 %copy-start = (bf16[4,4,160,128]{3,2,1,0:T(8,128)(2,1)S(1)}, bf16[4,4,160,128]{3,2,1,0:T(8,128)(2,1)}, u32[]{:S(2)}) copy-start(bf16[4,4,160,128]{3,2,1,0:T(8,128)(2,1)} %get-tuple-element.22) | copy-start | bytes 1966084
  62.2 1.3 %copy-start.2 = (f32[1152,128]{1,0:T(8,128)S(1)}, f32[1152,128]{1,0:T(8,128)}, u32[]{:S(2)}) copy-start(f32[1152,128]{1,0:T(8,128)} %get-tuple-element.13) | copy-start | bytes 1769476
  63.5 1.1 %copy-start.3 = (f32[384,128]{1,0:T(8,128)S(1)}, f32[384,128]{1,0:T(8,128)}, u32[]{:S(2)}) copy-start(f32[384,128]{1,0:T(8,128)} %get-tuple-element.14) | copy-start | bytes 589828

commit v3 on v2

--- a/solution.py
+++ b/solution.py
@@ -9,10 +9,13 @@
 from jax.sharding import PartitionSpec as P
 
 MESH = pl.DeviceIdType.MESH
+PAIR_WIRE = jnp.bfloat16
+PART_WIRE = jnp.bfloat16
+SUM_WIRE = jnp.bfloat16
 
 
 def at(start, size):
-    return pl.ds(pl.multiple_of(start, 8), size)
+    return pl.ds(pl.multiple_of(start, 16), size)
 
 
 def each(count, act):
@@ -94,11 +97,19 @@
     space_back,
     time_back,
     sums,
+    pair_out,
     pair_in,
     mid,
+    mid_out,
     shard_in,
     total,
+    out_f,
+    out_r,
+    grad_in,
+    grad_s,
+    grad_t,
     load_sem,
+    store_sem,
     send_sem,
     recv_sem,
 ):
@@ -246,11 +257,12 @@
         acts[frame + 2] = act.astype(jnp.bfloat16).reshape(height, width, channels)
 
     frames(0, count, convolve)
+    loads[1].wait()
+    loads[2].wait()
+    leave(2)
+    leave(3)
     launch(4)
     launch(5)
-
-    loads[1].wait()
-    loads[2].wait()
     arrive(2)
     arrive(3)
 
@@ -299,10 +311,11 @@
     def rows_to(step):
         return lax.rem(tile + step, tiles) * half
 
+    pair_out[...] = sums[...].astype(PAIR_WIRE)
     each(
         tiles,
         lambda step: remote(
-            sums.at[at(rows_to(step), half)], pair_in.at[step - 1], 8, tile_peer(step)
+            pair_out.at[at(rows_to(step), half)], pair_in.at[step - 1], 8, tile_peer(step)
         ).start(),
     )
 
@@ -310,7 +323,7 @@
         base = flat(cells[frame, pl.ds(1, height)]).astype(jnp.float32)
         causal = jnp.concatenate([flat(acts[frame + 2 - lag]) for lag in range(taps)], axis=1)
         anticausal = jnp.concatenate([flat(acts[frame + 2 + lag]) for lag in range(taps)], axis=1)
-        for joined, ref in ((causal, out_f_ref), (anticausal, out_r_ref)):
+        for joined, ref in ((causal, out_f), (anticausal, out_r)):
             value = base + jnp.dot(joined, time_ref[...], preferred_element_type=jnp.float32)
             ref[frame] = value.astype(jnp.bfloat16).reshape(height, width, channels)
 
@@ -320,17 +333,30 @@
         )
         value = flat(cot_f[frame]).astype(jnp.float32) + flat(cot_r[frame + 2]).astype(jnp.float32)
         value = value + across(joined, space_back[...])
-        grad_in_ref[frame] = value.astype(jnp.bfloat16).reshape(height, width, channels)
-
+        grad_in[frame] = value.astype(jnp.bfloat16).reshape(height, width, channels)
+
+    stores = [
+        pltpu.make_async_copy(src, dst, store_sem.at[index])
+        for index, (src, dst) in enumerate(
+            (
+                (out_f, out_f_ref),
+                (out_r, out_r_ref),
+                (grad_in, grad_in_ref),
+                (grad_s, grad_s_ref),
+                (grad_t, grad_t_ref),
+            )
+        )
+    ]
     settle(8, pair_in)
     own_half = sums[at(tile * half, half), :]
     for index in range(tiles - 1):
-        own_half = own_half + pair_in[index]
+        own_half = own_half + pair_in[index].astype(jnp.float32)
     mid[...] = own_half
+    mid_out[...] = own_half.astype(PART_WIRE)
     each(
         shards,
         lambda step: remote(
-            mid.at[at(lax.rem(shard + step, shards) * chunk, chunk)],
+            mid_out.at[at(lax.rem(shard + step, shards) * chunk, chunk)],
             shard_in.at[step - 1],
             9,
             shard_peer(step),
@@ -339,15 +365,17 @@
     arrive(4)
     arrive(5)
     frames(0, count, outputs)
+    stores[0].start()
+    stores[1].start()
     settle(9, shard_in)
     part = lax.fori_loop(
         0,
         shards - 1,
-        lambda index, value: value + shard_in[index],
+        lambda index, value: value + shard_in[index].astype(jnp.float32),
         mid[at(shard * chunk, chunk), :],
     )
     own = at(tile * half + shard * chunk, chunk)
-    total[own, :] = part * scale
+    total[own, :] = (part * scale).astype(SUM_WIRE)
     each(
         shards,
         lambda step: remote(total.at[own], total.at[own], 10, shard_peer(step)).start(),
@@ -359,18 +387,53 @@
         rim = spread(flat(rim_in[side]).astype(jnp.float32), edge, width)
         wide[:, row] = rim.reshape(count, width, taps * channels)
     frames(0, count, input_grads)
+    stores[2].start()
     settle(10, total.at[pl.ds(0, (shards - 1) * chunk)])
     mine = at(tile * half, half)
     each(
         tiles,
         lambda step: remote(total.at[mine], total.at[mine], 11, tile_peer(step)).start(),
     )
-    for index in range(8):
+    for index in (0, 1, 4, 5, 6, 7):
         leave(index)
     settle(11, total.at[pl.ds(0, (tiles - 1) * half)])
     split = taps * taps * channels
-    grad_s_ref[...] = total[:split, :]
-    grad_t_ref[...] = total[split : split + taps * channels, :]
+    grad_s[...] = total[:split, :].astype(jnp.float32)
+    stores[3].start()
+    grad_t[...] = total[split : split + taps * channels, :].astype(jnp.float32)
+    stores[4].start()
+    for store in stores:
+        store.wait()
+
+
+def deliver_kernel(*refs):
+    count = (len(refs) - 2) // 3
+    sources, targets, held = refs[:count], refs[count : 2 * count], refs[2 * count : 3 * count]
+    load_sem, store_sem = refs[3 * count :]
+    loads, stores = [], []
+    for index in range(count):
+        loads.append(pltpu.make_async_copy(sources[index], held[index], load_sem.at[index]))
+        stores.append(pltpu.make_async_copy(held[index], targets[index], store_sem.at[index]))
+    for load in loads:
+        load.start()
+    for load, store in zip(loads, stores):
+        load.wait()
+        store.start()
+    for store in stores:
+        store.wait()
+
+
+def deliver(*values):
+    hbm = pl.BlockSpec(memory_space=pl.ANY)
+    count = len(values)
+    return pl.pallas_call(
+        deliver_kernel,
+        out_shape=tuple(jax.ShapeDtypeStruct(value.shape, value.dtype) for value in values),
+        in_specs=[hbm] * count,
+        out_specs=(hbm,) * count,
+        scratch_shapes=[pltpu.VMEM(value.shape, value.dtype) for value in values]
+        + [pltpu.SemaphoreType.DMA((count,)), pltpu.SemaphoreType.DMA((count,))],
+    )(*values)
 
 
 def body(latent, cot_forward, cot_reverse, spatial_weight, temporal_weight):
@@ -379,14 +442,14 @@
     positions = count * height * width * shards * tiles
     scale = 1.0 / math.sqrt(positions)
     rows = 12 * channels
-    unit = 8 * tiles * shards
+    unit = 16 * tiles * shards
     padded = -(-rows // unit) * unit
     half = padded // tiles
     chunk = half // shards
     kind = jnp.bfloat16
     vmem = pl.BlockSpec(memory_space=pltpu.VMEM)
     hbm = pl.BlockSpec(memory_space=pl.ANY)
-    out_f, out_r, grad_in, grad_s, grad_t = pl.pallas_call(
+    results = pl.pallas_call(
         functools.partial(kernel, tiles, shards, scale),
         out_shape=(
             jax.ShapeDtypeStruct(latent.shape, kind),
@@ -396,7 +459,7 @@
             jax.ShapeDtypeStruct((3 * channels, channels), jnp.float32),
         ),
         in_specs=[hbm, hbm, hbm, vmem, vmem],
-        out_specs=(vmem, vmem, vmem, vmem, vmem),
+        out_specs=(hbm, hbm, hbm, hbm, hbm),
         scratch_shapes=[
             pltpu.VMEM((count, height + 2, width, channels), kind),
             pltpu.VMEM((count + 2, height, width, channels), kind),
@@ -410,11 +473,19 @@
             pltpu.VMEM((channels, 9 * channels), kind),
             pltpu.VMEM((channels, 6 * channels), kind),
             pltpu.VMEM((padded, channels), jnp.float32),
-            pltpu.VMEM((tiles - 1, half, channels), jnp.float32),
+            pltpu.VMEM((padded, channels), PAIR_WIRE),
+            pltpu.VMEM((tiles - 1, half, channels), PAIR_WIRE),
             pltpu.VMEM((half, channels), jnp.float32),
-            pltpu.VMEM((shards - 1, chunk, channels), jnp.float32),
-            pltpu.VMEM((padded, channels), jnp.float32),
+            pltpu.VMEM((half, channels), PART_WIRE),
+            pltpu.VMEM((shards - 1, chunk, channels), PART_WIRE),
+            pltpu.VMEM((padded, channels), SUM_WIRE),
+            pltpu.VMEM(latent.shape, kind),
+            pltpu.VMEM(latent.shape, kind),
+            pltpu.VMEM(latent.shape, kind),
+            pltpu.VMEM((9 * channels, channels), jnp.float32),
+            pltpu.VMEM((3 * channels, channels), jnp.float32),
             pltpu.SemaphoreType.DMA((3,)),
+            pltpu.SemaphoreType.DMA((5,)),
             pltpu.SemaphoreType.DMA((12,)),
             pltpu.SemaphoreType.DMA((12,)),
         ],
@@ -426,6 +497,7 @@
         spatial_weight.reshape(9 * channels, channels),
         temporal_weight.reshape(3 * channels, channels),
     )
+    out_f, out_r, grad_in, grad_s, grad_t = deliver(*results)
     return (
         out_f,
         out_r,

time: 66.4 us -> 51.8 us (0.78); the launches traced: 65.3 us -> 51.6 us
  Pallas kernels: 58.2 us -> 51 us
  local copies, waits for them, and re-layouts: 6.46 us -> 0 us
    pallas_call x1, Pallas kernels: 58.2 us -> 48.3 us  [body(): pl.pallas_call(functools.partial(kernel, tiles, shards, scale), out_shape...]
    unnamed x13 -> x0, local copies, waits for them, and re-layouts: 6.46 us -> none
    pallas_call x0 -> x1, Pallas kernels: none -> 2.69 us  [deliver(): pl.pallas_call(deliver_kernel, out_shape=tuple((jax.ShapeDtypeStruct(valu...]
where the time goes in v3:
time: 51.8 us; the launch traced here: 51.6 us
  Pallas kernels  51 us (98%)
  between operations  0.64 us (1%)
    pallas_call x1, Pallas kernels, body(): pl.pallas_call(functools.partial(kernel, tiles, shards, scale), out_shape...  48.3 us
    pallas_call x1, Pallas kernels, deliver(): pl.pallas_call(deliver_kernel, out_shape=tuple((jax.ShapeDtypeStruct(valu...  2.69 us

profile of v3, /device:TPU:0, one launch (start us, length us, event | category | flops | bytes accessed | tf_op | source)
XLA Modules:
  0.0 51.6 jit_solution(2147058611632572168)
XLA Ops:
  0.6 48.3 %shard_map.92 = (bf16[4,4,160,128]{3,2,1,0:T(8,128)(2,1)}, bf16[4,4,160,128]{3,2,1,0:T(8,128)(2,1)}, bf16[4,4,160,128]{3,2,1,0:T(8,128)(2,1)}, f32[1152,128]{1,0:T(8,128)}, f32[384,128]{1,0:T(8,128)}) custom-call(bf16[4,4,160,128]{3,2,1,0:T(8,128)(2,1)} %latent_ref.1, bf16[4,4,160,128]{3,2,1,0:T(8,128)(2,1)} %fwd_ref.1, bf16[4,4,160,128]{3,2,1,0:T(8,128)(2,1)} %rev_ref.1, ...), custom_call_target="tpu_custom_call" | custom-call | tf_op jit(solution)/shard_map/pallas_call | solution.py:452
  48.9 2.7 %shard_map.93 = (bf16[4,4,160,128]{3,2,1,0:T(8,128)(2,1)}, bf16[4,4,160,128]{3,2,1,0:T(8,128)(2,1)}, bf16[4,4,160,128]{3,2,1,0:T(8,128)(2,1)}, f32[1152,128]{1,0:T(8,128)}, f32[384,128]{1,0:T(8,128)}) custom-call(bf16[4,4,160,128]{3,2,1,0:T(8,128)(2,1)} %get-tuple-element.15.refs_0_, bf16[4,4,160,128]{3,2,1,0:T(8,128)(2,1)} %get-tuple-element.16.refs_1_, ...), custom_call_target="tpu_custom_call" | custom-call | tf_op jit(solution)/shard_map/pallas_call | solution.py:429

commit v4 on v3

--- a/solution.py
+++ b/solution.py
@@ -9,9 +9,12 @@
 from jax.sharding import PartitionSpec as P
 
 MESH = pl.DeviceIdType.MESH
-PAIR_WIRE = jnp.bfloat16
-PART_WIRE = jnp.bfloat16
+PAIR_WIRE = jnp.float32
+PART_WIRE = jnp.float32
 SUM_WIRE = jnp.bfloat16
+FIRST = 0
+MOMENT = 2
+LATE_OUT = False
 
 
 def at(start, size):
@@ -155,39 +158,23 @@
 
     next_tile, last_tile = tile_peer(1), tile_peer(tiles - 1)
     next_shard, last_shard = shard_peer(1), shard_peer(shards - 1)
+    up = (next_tile, has_next_tile, has_last_tile)
+    down = (last_tile, has_last_tile, has_next_tile)
+    later = (next_shard, has_next_shard, has_last_shard)
+    earlier = (last_shard, has_last_shard, has_next_shard)
     moves = [
-        (latent_ref.at[:, height - 1], cells.at[:, 0], next_tile, has_next_tile, has_last_tile),
-        (latent_ref.at[:, 0], cells.at[:, height + 1], last_tile, has_last_tile, has_next_tile),
-        (
-            fwd_ref.at[pl.ds(0, 2)],
-            cot_f.at[pl.ds(count, 2)],
-            last_shard,
-            has_last_shard,
-            has_next_shard,
-        ),
-        (
-            rev_ref.at[pl.ds(count - 2, 2)],
-            cot_r.at[pl.ds(0, 2)],
-            next_shard,
-            has_next_shard,
-            has_last_shard,
-        ),
-        (
-            acts.at[pl.ds(count, 2)],
-            acts.at[pl.ds(0, 2)],
-            next_shard,
-            has_next_shard,
-            has_last_shard,
-        ),
-        (
-            acts.at[pl.ds(2, 2)],
-            acts.at[pl.ds(count + 2, 2)],
-            last_shard,
-            has_last_shard,
-            has_next_shard,
-        ),
-        (rim_out.at[1], rim_in.at[0], next_tile, has_next_tile, has_last_tile),
-        (rim_out.at[0], rim_in.at[1], last_tile, has_last_tile, has_next_tile),
+        (latent_ref.at[:, height - 1], cells.at[:, 0], *up),
+        (latent_ref.at[:, 0], cells.at[:, height + 1], *down),
+        (fwd_ref.at[0], cot_f.at[count], *earlier),
+        (rev_ref.at[count - 1], cot_r.at[1], *later),
+        (fwd_ref.at[1], cot_f.at[count + 1], *earlier),
+        (rev_ref.at[count - 2], cot_r.at[0], *later),
+        (acts.at[count + 1], acts.at[1], *later),
+        (acts.at[2], acts.at[count + 2], *earlier),
+        (acts.at[count], acts.at[0], *later),
+        (acts.at[3], acts.at[count + 3], *earlier),
+        (rim_out.at[1], rim_in.at[0], *up),
+        (rim_out.at[0], rim_in.at[1], *down),
     ]
     copies = [remote(src, dst, index, peer) for index, (src, dst, peer, _, _) in enumerate(moves)]
 
@@ -200,20 +187,12 @@
     def leave(index):
         pl.when(moves[index][3])(copies[index].wait_send)
 
-    for index in range(8):
-        if index < 6:
-            target = moves[index][1]
-
-            @pl.when(jnp.logical_not(moves[index][4]))
-            def _(target=target):
-                target[...] = jnp.zeros(target.shape, target.dtype)
-
-        else:
-            target = rim_in.at[index - 6]
-
-            @pl.when(jnp.logical_not(moves[index][4]))
-            def _(target=target):
-                target[...] = jnp.zeros(target.shape, target.dtype)
+    for index in range(len(moves)):
+        target = moves[index][1]
+
+        @pl.when(jnp.logical_not(moves[index][4]))
+        def _(target=target):
+            target[...] = jnp.zeros(target.shape, target.dtype)
 
     sums[...] = jnp.zeros_like(sums)
     for row in range(taps):
@@ -232,7 +211,7 @@
             space_back[:, index * channels : (index + 1) * channels] = weight
 
     pl.semaphore_wait(barrier, tiles + shards - 2)
-    for index in range(4):
+    for index in range(6):
         launch(index)
     place = columns(plane, width, channels)
 
@@ -257,14 +236,14 @@
         acts[frame + 2] = act.astype(jnp.bfloat16).reshape(height, width, channels)
 
     frames(0, count, convolve)
-    loads[1].wait()
-    loads[2].wait()
-    leave(2)
-    leave(3)
-    launch(4)
-    launch(5)
-    arrive(2)
-    arrive(3)
+
+    def second_acts(moment):
+        if moment == FIRST:
+            launch(6)
+            launch(7)
+        if moment == MOMENT:
+            launch(8)
+            launch(9)
 
     def backward(frame):
         joined = jnp.concatenate(
@@ -297,9 +276,20 @@
                     row * channels : (row + 1) * channels, col * channels : (col + 1) * channels
                 ]
 
-    frames(0, count, backward)
-    launch(6)
-    launch(7)
+    loads[1].wait()
+    loads[2].wait()
+    arrive(2)
+    arrive(3)
+    frames(1, count - 1, backward)
+    for index in (2, 3, 4, 5):
+        leave(index)
+    second_acts(0)
+    arrive(4)
+    arrive(5)
+    backward(0)
+    backward(count - 1)
+    launch(10)
+    launch(11)
 
     half = sums.shape[0] // tiles
     chunk = half // shards
@@ -315,9 +305,11 @@
     each(
         tiles,
         lambda step: remote(
-            pair_out.at[at(rows_to(step), half)], pair_in.at[step - 1], 8, tile_peer(step)
+            pair_out.at[at(rows_to(step), half)], pair_in.at[step - 1], 12, tile_peer(step)
         ).start(),
     )
+
+    second_acts(1)
 
     def outputs(frame):
         base = flat(cells[frame, pl.ds(1, height)]).astype(jnp.float32)
@@ -326,6 +318,13 @@
         for joined, ref in ((causal, out_f), (anticausal, out_r)):
             value = base + jnp.dot(joined, time_ref[...], preferred_element_type=jnp.float32)
             ref[frame] = value.astype(jnp.bfloat16).reshape(height, width, channels)
+
+    def all_outputs():
+        for index in range(6, 10):
+            arrive(index)
+        frames(0, count, outputs)
+        stores[0].start()
+        stores[1].start()
 
     def input_grads(frame):
         joined = jnp.concatenate(
@@ -347,7 +346,7 @@
             )
         )
     ]
-    settle(8, pair_in)
+    settle(12, pair_in)
     own_half = sums[at(tile * half, half), :]
     for index in range(tiles - 1):
         own_half = own_half + pair_in[index].astype(jnp.float32)
@@ -358,16 +357,12 @@
         lambda step: remote(
             mid_out.at[at(lax.rem(shard + step, shards) * chunk, chunk)],
             shard_in.at[step - 1],
-            9,
+            13,
             shard_peer(step),
         ).start(),
     )
-    arrive(4)
-    arrive(5)
-    frames(0, count, outputs)
-    stores[0].start()
-    stores[1].start()
-    settle(9, shard_in)
+    second_acts(2)
+    settle(13, shard_in)
     part = lax.fori_loop(
         0,
         shards - 1,
@@ -378,25 +373,30 @@
     total[own, :] = (part * scale).astype(SUM_WIRE)
     each(
         shards,
-        lambda step: remote(total.at[own], total.at[own], 10, shard_peer(step)).start(),
-    )
-    arrive(6)
-    arrive(7)
+        lambda step: remote(total.at[own], total.at[own], 14, shard_peer(step)).start(),
+    )
+    second_acts(3)
+    arrive(10)
+    arrive(11)
     edge = columns(count * width, width, channels)
     for side, row in ((0, 0), (1, height + 1)):
         rim = spread(flat(rim_in[side]).astype(jnp.float32), edge, width)
         wide[:, row] = rim.reshape(count, width, taps * channels)
     frames(0, count, input_grads)
     stores[2].start()
-    settle(10, total.at[pl.ds(0, (shards - 1) * chunk)])
+    if not LATE_OUT:
+        all_outputs()
+    settle(14, total.at[pl.ds(0, (shards - 1) * chunk)])
     mine = at(tile * half, half)
     each(
         tiles,
-        lambda step: remote(total.at[mine], total.at[mine], 11, tile_peer(step)).start(),
-    )
-    for index in (0, 1, 4, 5, 6, 7):
+        lambda step: remote(total.at[mine], total.at[mine], 15, tile_peer(step)).start(),
+    )
+    if LATE_OUT:
+        all_outputs()
+    for index in (0, 1, 6, 7, 8, 9, 10, 11):
         leave(index)
-    settle(11, total.at[pl.ds(0, (tiles - 1) * half)])
+    settle(15, total.at[pl.ds(0, (tiles - 1) * half)])
     split = taps * taps * channels
     grad_s[...] = total[:split, :].astype(jnp.float32)
     stores[3].start()
@@ -486,8 +486,8 @@
             pltpu.VMEM((3 * channels, channels), jnp.float32),
             pltpu.SemaphoreType.DMA((3,)),
             pltpu.SemaphoreType.DMA((5,)),
-            pltpu.SemaphoreType.DMA((12,)),
-            pltpu.SemaphoreType.DMA((12,)),
+            pltpu.SemaphoreType.DMA((16,)),
+            pltpu.SemaphoreType.DMA((16,)),
         ],
         compiler_params=pltpu.CompilerParams(collective_id=0, has_side_effects=True),
     )(

time: 51.8 us -> 52.4 us (1.012)
  no operation moved by 1% of the time
where the time goes in v4:
time: 52.4 us; the launch traced here: 51.8 us
  Pallas kernels  51.1 us (98%)
  between operations  0.64 us (1%)
    pallas_call x1, Pallas kernels, body(): pl.pallas_call(functools.partial(kernel, tiles, shards, scale), out_shape...  48.4 us
    pallas_call x1, Pallas kernels, deliver(): pl.pallas_call(deliver_kernel, out_shape=tuple((jax.ShapeDtypeStruct(valu...  2.69 us

profile of v4, /device:TPU:0, one launch (start us, length us, event | category | flops | bytes accessed | tf_op | source)
XLA Modules:
  0.0 51.8 jit_solution(10779944741335819189)
XLA Ops:
  0.6 48.4 %shard_map.92 = (bf16[4,4,160,128]{3,2,1,0:T(8,128)(2,1)}, bf16[4,4,160,128]{3,2,1,0:T(8,128)(2,1)}, bf16[4,4,160,128]{3,2,1,0:T(8,128)(2,1)}, f32[1152,128]{1,0:T(8,128)}, f32[384,128]{1,0:T(8,128)}) custom-call(bf16[4,4,160,128]{3,2,1,0:T(8,128)(2,1)} %latent_ref.1, bf16[4,4,160,128]{3,2,1,0:T(8,128)(2,1)} %fwd_ref.1, bf16[4,4,160,128]{3,2,1,0:T(8,128)(2,1)} %rev_ref.1, ...), custom_call_target="tpu_custom_call" | custom-call | tf_op jit(solution)/shard_map/pallas_call | solution.py:452
  49.1 2.7 %shard_map.93 = (bf16[4,4,160,128]{3,2,1,0:T(8,128)(2,1)}, bf16[4,4,160,128]{3,2,1,0:T(8,128)(2,1)}, bf16[4,4,160,128]{3,2,1,0:T(8,128)(2,1)}, f32[1152,128]{1,0:T(8,128)}, f32[384,128]{1,0:T(8,128)}) custom-call(bf16[4,4,160,128]{3,2,1,0:T(8,128)(2,1)} %get-tuple-element.15.refs_0_, bf16[4,4,160,128]{3,2,1,0:T(8,128)(2,1)} %get-tuple-element.16.refs_1_, ...), custom_call_target="tpu_custom_call" | custom-call | tf_op jit(solution)/shard_map/pallas_call | solution.py:429

commit v5 on v4

--- a/solution.py
+++ b/solution.py
@@ -10,7 +10,7 @@
 
 MESH = pl.DeviceIdType.MESH
 PAIR_WIRE = jnp.float32
-PART_WIRE = jnp.float32
+PART_WIRE = jnp.bfloat16
 SUM_WIRE = jnp.bfloat16
 FIRST = 0
 MOMENT = 2

time: 52.4 us -> 50.3 us (0.960)
  Pallas kernels: 51.1 us -> 48.8 us
    pallas_call x1, Pallas kernels: 48.4 us -> 46.1 us  [body(): pl.pallas_call(functools.partial(kernel, tiles, shards, scale), out_shape...]
where the time goes in v5:
time: 50.3 us; the launch traced here: 49.5 us
  Pallas kernels  48.8 us (97%)
  between operations  0.64 us (1%)
    pallas_call x1, Pallas kernels, body(): pl.pallas_call(functools.partial(kernel, tiles, shards, scale), out_shape...  46.1 us
    pallas_call x1, Pallas kernels, deliver(): pl.pallas_call(deliver_kernel, out_shape=tuple((jax.ShapeDtypeStruct(valu...  2.69 us

profile of v5, /device:TPU:0, one launch (start us, length us, event | category | flops | bytes accessed | tf_op | source)
XLA Modules:
  0.0 49.5 jit_solution(6812911555764266584)
XLA Ops:
  0.6 46.1 %shard_map.92 = (bf16[4,4,160,128]{3,2,1,0:T(8,128)(2,1)}, bf16[4,4,160,128]{3,2,1,0:T(8,128)(2,1)}, bf16[4,4,160,128]{3,2,1,0:T(8,128)(2,1)}, f32[1152,128]{1,0:T(8,128)}, f32[384,128]{1,0:T(8,128)}) custom-call(bf16[4,4,160,128]{3,2,1,0:T(8,128)(2,1)} %latent_ref.1, bf16[4,4,160,128]{3,2,1,0:T(8,128)(2,1)} %fwd_ref.1, bf16[4,4,160,128]{3,2,1,0:T(8,128)(2,1)} %rev_ref.1, ...), custom_call_target="tpu_custom_call" | custom-call | tf_op jit(solution)/shard_map/pallas_call | solution.py:452
  46.8 2.7 %shard_map.93 = (bf16[4,4,160,128]{3,2,1,0:T(8,128)(2,1)}, bf16[4,4,160,128]{3,2,1,0:T(8,128)(2,1)}, bf16[4,4,160,128]{3,2,1,0:T(8,128)(2,1)}, f32[1152,128]{1,0:T(8,128)}, f32[384,128]{1,0:T(8,128)}) custom-call(bf16[4,4,160,128]{3,2,1,0:T(8,128)(2,1)} %get-tuple-element.15.refs_0_, bf16[4,4,160,128]{3,2,1,0:T(8,128)(2,1)} %get-tuple-element.16.refs_1_, ...), custom_call_target="tpu_custom_call" | custom-call | tf_op jit(solution)/shard_map/pallas_call | solution.py:429
